TPU v7x, 1024 devices: a whole 8x8x8 slice. The times are simulated.
1024 devices in a mesh: row: 16 (over y, z_lo), col: 64 (over x, z_hi, core).
Axes of the slice: x: 8, y: 8, z: 8 (z_hi: 4, z_lo: 2; z = z_hi * 2 + z_lo), core: 2. Of those that a mesh axis runs over, the one named last changes fastest.
Arguments:
- fields: float32 [5, 1, 4096, 2048], P(None, None, 'col', 'row'), may hold values from -3 to 150, as said below
Outputs:
- updated: float32 [5, 1, 4096, 2048], P(None, None, 'col', 'row')
Inputs may be any that keep to these rules, and one draw needn't show every extreme that they name: `fields`: field 0 is the density and field 4 the total energy; density and pressure are positive in every cell.
All inputs are finite; a program needn't handle non-finite values.
Results may differ from a plain program's by a relative error of at most 0.0003.
Values sent between devices are 32-bit elements; how exact they have to be, the bound alone decides.
No kernel may reach another device: no remote copies, remote signals or barrier semaphores. Data moves between devices by JAX's collectives and lax.ppermute only.
A program may use at most 32 MiB of HBM per device.

v0:
```python
import jax
import jax.numpy as jnp
from jax import lax
from jax.sharding import Mesh
from jax.sharding import PartitionSpec as P

ROW_COL = ("row_0", "row_1", "col_0", "col_1", "col_2")
ROW = ("row_0", "row_1")
COL = ("col_0", "col_1", "col_2")


GAMMA = 1.4
COURANT = 0.3


def one_axis_at_a_time(shard, axes):
    for axis in axes:
        shard = lax.pmax(shard, axis)
    return shard


def extended(shard, sides, width):
    for axis, dim in sides:
        count, length = (lax.axis_size(axis), shard.shape[dim])
        up = [(i, (i + 1) % count) for i in range(count)]
        down = [(j, i) for i, j in up]
        last = lax.slice_in_dim(shard, length - width, length, axis=dim)
        leading = lax.slice_in_dim(shard, 0, width, axis=dim)
        before = lax.ppermute(last, axis, up)
        after = lax.ppermute(leading, axis, down)
        shard = jnp.concatenate([before, shard, after], axis=dim)
    return shard


def window_slice(profile, begin_at, trim_end, direction_axis):
    direction_axis = direction_axis % profile.ndim
    return lax.slice_in_dim(
        profile, begin_at, profile.shape[direction_axis] - trim_end, axis=direction_axis
    )


def minmod(first_slope, second_slope):
    return (
        0.5
        * (jnp.sign(first_slope) + jnp.sign(second_slope))
        * jnp.minimum(jnp.abs(first_slope), jnp.abs(second_slope))
    )


def rebuild(profile, direction_axis):
    far_left = window_slice(profile, 0, 3, direction_axis)
    near_left = window_slice(profile, 1, 2, direction_axis)
    near_right = window_slice(profile, 2, 1, direction_axis)
    far_right = window_slice(profile, 3, 0, direction_axis)
    edge_value = 7.0 / 12.0 * (near_left + near_right) - 1.0 / 12.0 * (far_left + far_right)
    edge_value = jnp.clip(
        edge_value, jnp.minimum(near_left, near_right), jnp.maximum(near_left, near_right)
    )
    centre = window_slice(profile, 2, 2, direction_axis)
    lower_edge = window_slice(edge_value, 0, 1, direction_axis)
    upper_edge = window_slice(edge_value, 1, 0, direction_axis)
    upper_jump = upper_edge - centre
    lower_jump = centre - lower_edge
    right_face = centre + minmod(upper_jump, 2.0 * lower_jump)
    left_face = centre - minmod(lower_jump, 2.0 * upper_jump)
    return (
        window_slice(right_face, 0, 1, direction_axis),
        window_slice(left_face, 1, 0, direction_axis),
    )


def face_terms(density, velocity, pressure, normal):
    speed_square = velocity[0] * velocity[0] + velocity[1] * velocity[1] + velocity[2] * velocity[2]
    energy = pressure / (GAMMA - 1.0) + 0.5 * density * speed_square
    normal_speed = velocity[normal - 1]
    conserved = [
        density,
        density * velocity[0],
        density * velocity[1],
        density * velocity[2],
        energy,
    ]
    face_flux = [density * normal_speed]
    for component in range(3):
        momentum_flux = density * normal_speed * velocity[component]
        if component == normal - 1:
            momentum_flux = momentum_flux + pressure
        face_flux.append(momentum_flux)
    face_flux.append(normal_speed * (energy + pressure))
    signal = jnp.abs(normal_speed) + jnp.sqrt(GAMMA * pressure / density)
    return (conserved, face_flux, signal)


def primitives(cells):
    density = cells[0]
    velocity = [cells[1] / density, cells[2] / density, cells[3] / density]
    kinetic = (
        0.5
        * density
        * (velocity[0] * velocity[0] + velocity[1] * velocity[1] + velocity[2] * velocity[2])
    )
    pressure = (GAMMA - 1.0) * (cells[4] - kinetic)
    return (density, velocity, pressure)


def courant(cells):
    density, velocity, pressure = primitives(cells)
    return jnp.maximum(jnp.abs(velocity[0]), jnp.abs(velocity[1])) + jnp.sqrt(
        GAMMA * pressure / density
    )


def sweep_along(padded, time_step, direction_axis, normal):
    density, velocity, pressure = primitives(padded)
    face_pairs = [
        rebuild(profile, direction_axis)
        for profile in [density, velocity[0], velocity[1], velocity[2], pressure]
    ]
    left_states = [pair[0] for pair in face_pairs]
    right_states = [pair[1] for pair in face_pairs]
    left_conserved, left_flux, left_signal = face_terms(
        left_states[0], left_states[1:4], left_states[4], normal
    )
    right_conserved, right_flux, right_signal = face_terms(
        right_states[0], right_states[1:4], right_states[4], normal
    )
    signal = jnp.maximum(left_signal, right_signal)
    results = []
    for component in range(5):
        face_flux = 0.5 * (left_flux[component] + right_flux[component]) - 0.5 * signal * (
            right_conserved[component] - left_conserved[component]
        )
        difference = window_slice(face_flux, 1, 0, direction_axis) - window_slice(
            face_flux, 0, 1, direction_axis
        )
        results.append(
            window_slice(padded[component], 3, 3, direction_axis) - time_step * difference
        )
    return jnp.stack(results)


def local(fields):
    local_peak = jnp.max(courant(fields))
    peak_speed = one_axis_at_a_time(local_peak, ROW_COL)
    time_step = COURANT / peak_speed
    padded = extended(fields, ((ROW, 3),), 3)
    block_fields = sweep_along(padded, time_step, -1, 1)
    padded = extended(block_fields, ((COL, 2),), 3)
    return sweep_along(padded, time_step, -2, 2)


def solution(mesh):
    split = Mesh(mesh.devices.reshape(8, 2, 8, 4, 2), ("row_0", "row_1", "col_0", "col_1", "col_2"))
    placed = (P(None, None, COL, ROW),)
    return jax.shard_map(
        local, mesh=split, in_specs=placed, out_specs=P(None, None, COL, ROW), check_vma=False
    )
```

profile of v0, /device:TPU:1, one launch (start us, length us, event | category | flops | bytes accessed | tf_op | source)
XLA Modules:
  0.0 92.8 jit_solution(11500466895732703123)
XLA Ops:
  0.0 0.0 copy-start
  0.0 1.2 %fusion.99 = (f32[5,1,64,3]{3,2,1,0:T(8,128)S(1)}, f32[5,1,64,3]{3,2,1,0:T(8,128)S(1)}) fusion(f32[5,1,64,128]{3,2,1,0:T(8,128)} %param.1), kind=kLoop, calls=%fused_computation.204 | loop fusion | bytes 15360 | tf_op jit(solution)/shard_map/slice | solution.py:27
  1.2 5.7 %collective-permute-start = (f32[5,1,64,3]{3,2,1,0:T(8,128)S(1)}, f32[5,1,64,3]{3,2,1,0:T(8,128)S(1)}, u32[]{:S(2)}, u32[]{:S(2)}) collective-permute-start(f32[5,1,64,3]{3,2,1,0:T(8,128)S(1)} %get-tuple-element.47), channel_id=1, source_target_pairs={{0,64},{64,128},{128,192},{192,256},{256,320},{320,384},{384,448},... | collective-permute-start | bytes 11528 | tf_op jit(solution)/shard_map/ppermute | solution.py:29
  6.9 5.6 %collective-permute-start.1 = (f32[5,1,64,3]{3,2,1,0:T(8,128)S(1)}, f32[5,1,64,3]{3,2,1,0:T(8,128)S(1)}, u32[]{:S(2)}, u32[]{:S(2)}) collective-permute-start(f32[5,1,64,3]{3,2,1,0:T(8,128)S(1)} %get-tuple-element.48), channel_id=1, source_target_pairs={{64,0},{128,64},{192,128},{256,192},{320,256},{384,320},{448,384},... | collective-permute-start | bytes 11528 | tf_op jit(solution)/shard_map/ppermute | solution.py:30
  12.5 0.0 copy-done
  12.5 0.6 add_reduce_fusion
  13.2 12.2 %pmax.35 = f32[]{:T(128)} all-reduce(f32[]{:T(128)} %add_reduce_fusion), channel_id=1, replica_groups=mesh['row_0'=8,'row_1'=2,'col_0'=8,'col_1'=4,'col_2'=2] {'row_0'}, use_global_device_ids=true, to_apply=%region_1.0 | all-reduce | flops 1 | bytes 8 | tf_op jit(solution)/shard_map/pmax | solution.py:18
  25.4 4.7 %pmax.36 = f32[]{:T(128)} all-reduce(f32[]{:T(128)} %pmax.35), channel_id=1, replica_groups=mesh['row_0'=8,'row_1'=2,'col_0'=8,'col_1'=4,'col_2'=2] {'row_1'}, use_global_device_ids=true, to_apply=%region_2.0 | all-reduce | flops 1 | bytes 8 | tf_op jit(solution)/shard_map/pmax | solution.py:18
  30.1 13.6 %pmax.37 = f32[]{:T(128)} all-reduce(f32[]{:T(128)} %pmax.36), channel_id=1, replica_groups=mesh['row_0'=8,'row_1'=2,'col_0'=8,'col_1'=4,'col_2'=2] {'col_0'}, use_global_device_ids=true, to_apply=%region_3.0 | all-reduce | flops 1 | bytes 8 | tf_op jit(solution)/shard_map/pmax | solution.py:18
  43.7 20.8 %pmax.38 = f32[]{:T(128)} all-reduce(f32[]{:T(128)} %pmax.37), channel_id=1, replica_groups=mesh['row_0'=8,'row_1'=2,'col_0'=8,'col_1'=4,'col_2'=2] {'col_1'}, use_global_device_ids=true, to_apply=%region_4.0 | all-reduce | flops 1 | bytes 8 | tf_op jit(solution)/shard_map/pmax | solution.py:18
  64.5 14.3 %pmax.39 = f32[]{:T(128)} all-reduce(f32[]{:T(128)} %pmax.38), channel_id=1, replica_groups=mesh['row_0'=8,'row_1'=2,'col_0'=8,'col_1'=4,'col_2'=2] {'col_2'}, use_global_device_ids=true, to_apply=%region_5.0 | all-reduce | flops 1 | bytes 8 | tf_op jit(solution)/shard_map/pmax | solution.py:18
  79.6 0.0 collective-permute-done
  79.6 0.0 collective-permute-done.1
  79.6 0.2 pad_maximum_fusion
  79.9 0.1 fusion.3
  80.0 0.1 fusion.7
  80.1 0.1 fusion.11
  80.3 0.1 fusion.15
  80.4 0.1 fusion.19
  80.5 0.1 slice_subtract_fusion.14
  80.6 0.1 slice_subtract_fusion.2
  80.8 0.1 slice_subtract_fusion.8
  80.9 0.6 multiply_subtract_fusion
  81.5 0.3 multiply_subtract_fusion.1
  81.9 0.1 fusion.79
  82.0 0.1 fusion.75
  82.1 0.1 fusion.71
  82.2 0.1 fusion.67
  82.3 0.1 fusion.63
  82.4 1.9 %collective-permute-start.2 = (f32[5,1,3,128]{3,2,1,0:T(4,128)S(1)}, f32[5,1,3,128]{3,2,1,0:T(4,128)S(1)}, u32[]{:S(2)}, u32[]{:S(2)}) collective-permute-start(f32[5,1,3,128]{3,2,1,0:T(4,128)S(1)} %get-tuple-element.45), channel_id=1, source_target_pairs={{0,1},{1,2},{2,3},{3,4},{4,5},{5,6},{6,7},{7,8},{8,9},{9,10},{10,1... | collective-permute-start | bytes 23048 | tf_op jit(solution)/shard_map/ppermute | solution.py:29
  84.3 2.4 %collective-permute-start.3 = (f32[5,1,3,128]{3,2,1,0:T(4,128)S(1)}, f32[5,1,3,128]{3,2,1,0:T(4,128)S(1)}, u32[]{:S(2)}, u32[]{:S(2)}) collective-permute-start(f32[5,1,3,128]{3,2,1,0:T(4,128)S(1)} %get-tuple-element.46), channel_id=1, source_target_pairs={{1,0},{2,1},{3,2},{4,3},{5,4},{6,5},{7,6},{8,7},{9,8},{10,9},{11,1... | collective-permute-start | bytes 23048 | tf_op jit(solution)/shard_map/ppermute | solution.py:30
  86.7 0.0 collective-permute-done.2
  86.7 3.8 %collective-permute-done.3 = f32[5,1,3,128]{3,2,1,0:T(4,128)S(1)} collective-permute-done((f32[5,1,3,128]{3,2,1,0:T(4,128)S(1)}, f32[5,1,3,128]{3,2,1,0:T(4,128)S(1)}, u32[]{:S(2)}, u32[]{:S(2)}) %collective-permute-start.3) | collective-permute-done | bytes 7712 | tf_op jit(solution)/shard_map/ppermute | solution.py:30
  90.8 0.4 multiply_subtract_fusion.5
  91.2 0.2 multiply_subtract_fusion.6
  91.5 0.0 copy-start.1
  91.5 0.7 copy-done.1
  92.2 0.6 fusion.43
  (20 shorter events, 0.4 us)
Async XLA Ops:
  0.0 12.5 %copy-start = (f32[5,1,64,128]{3,2,1,0:T(8,128)S(1)}, f32[5,1,64,128]{3,2,1,0:T(8,128)}, u32[]{:S(2)}) copy-start(f32[5,1,64,128]{3,2,1,0:T(8,128)} %param.1) | copy-start | bytes 491524
  1.2 78.4 %collective-permute-start = (f32[5,1,64,3]{3,2,1,0:T(8,128)S(1)}, f32[5,1,64,3]{3,2,1,0:T(8,128)S(1)}, u32[]{:S(2)}, u32[]{:S(2)}) collective-permute-start(f32[5,1,64,3]{3,2,1,0:T(8,128)S(1)} %get-tuple-element.47), channel_id=1, source_target_pairs={{0,64},{64,128},{128,192},{192,256},{256,320},{320,384},{384,448},... | collective-permute-start | bytes 11528 | tf_op jit(solution)/shard_map/ppermute | solution.py:29
  6.9 72.7 %collective-permute-start.1 = (f32[5,1,64,3]{3,2,1,0:T(8,128)S(1)}, f32[5,1,64,3]{3,2,1,0:T(8,128)S(1)}, u32[]{:S(2)}, u32[]{:S(2)}) collective-permute-start(f32[5,1,64,3]{3,2,1,0:T(8,128)S(1)} %get-tuple-element.48), channel_id=1, source_target_pairs={{64,0},{128,64},{192,128},{256,192},{320,256},{384,320},{448,384},... | collective-permute-start | bytes 11528 | tf_op jit(solution)/shard_map/ppermute | solution.py:30
  82.4 4.3 %collective-permute-start.2 = (f32[5,1,3,128]{3,2,1,0:T(4,128)S(1)}, f32[5,1,3,128]{3,2,1,0:T(4,128)S(1)}, u32[]{:S(2)}, u32[]{:S(2)}) collective-permute-start(f32[5,1,3,128]{3,2,1,0:T(4,128)S(1)} %get-tuple-element.45), channel_id=1, source_target_pairs={{0,1},{1,2},{2,3},{3,4},{4,5},{5,6},{6,7},{7,8},{8,9},{9,10},{10,1... | collective-permute-start | bytes 23048 | tf_op jit(solution)/shard_map/ppermute | solution.py:29
  84.3 6.2 %collective-permute-start.3 = (f32[5,1,3,128]{3,2,1,0:T(4,128)S(1)}, f32[5,1,3,128]{3,2,1,0:T(4,128)S(1)}, u32[]{:S(2)}, u32[]{:S(2)}) collective-permute-start(f32[5,1,3,128]{3,2,1,0:T(4,128)S(1)} %get-tuple-element.46), channel_id=1, source_target_pairs={{1,0},{2,1},{3,2},{4,3},{5,4},{6,5},{7,6},{8,7},{9,8},{10,9},{11,1... | collective-permute-start | bytes 23048 | tf_op jit(solution)/shard_map/ppermute | solution.py:30
  91.5 0.7 copy-start.1
where the time goes:
time: 94.2 us; the launch traced here: 92.8 us
  blocking collectives  65.7 us (70%)
  starting transfers between devices  15.7 us (17%)
  other arithmetic  4.75 us (5%)
  waiting for transfers between devices  3.77 us (4%)
  local copies, waits for them, and re-layouts  1.87 us (2%)
  between operations  1.03 us (1%)
    pmax x5, blocking collectives, one_axis_at_a_time(): shard = lax.pmax(shard, axis)  65.7 us
    ppermute x2, starting transfers between devices, extended(): after = lax.ppermute(leading, axis, down)  8.03 us
    ppermute x2, starting transfers between devices, extended(): before = lax.ppermute(last, axis, up)  7.65 us
    ppermute x2, waiting for transfers between devices, extended(): after = lax.ppermute(leading, axis, down)  3.76 us
  transfers between devices with their start and end apart: 4, of which 1 were waited for; matrix products, arithmetic and copies ran while one was open for 1% of the time, Pallas kernels for 0%

commit v1 on v0

v1 whole, which is shorter than its diff:
```python
import jax
import jax.numpy as jnp
from jax import lax
from jax.experimental import pallas as pl
from jax.experimental.pallas import tpu as pltpu
from jax.sharding import Mesh
from jax.sharding import PartitionSpec as P

ROW = ("row_0", "row_1")
COL = ("col_0", "col_1", "col_2")

GAMMA = 1.4
COURANT = 0.3
WIDTH = 3
FIELDS = 5
PACKED = 16
VMEM = pl.BlockSpec(memory_space=pltpu.VMEM)
SMEM = pl.BlockSpec(memory_space=pltpu.SMEM)


def minmod(first, second):
    low = jnp.minimum(first, second)
    high = jnp.maximum(first, second)
    return jnp.maximum(low, 0.0) + jnp.minimum(high, 0.0)


def shifted(profile, step, axis):
    return pltpu.roll(profile, (-step) % profile.shape[axis], axis)


def primitives(cells):
    inverse = 1.0 / cells[0]
    velocity = [cells[k] * inverse for k in (1, 2, 3)]
    kinetic = 0.5 * (cells[1] * velocity[0] + cells[2] * velocity[1] + cells[3] * velocity[2])
    return [cells[0], *velocity, (GAMMA - 1.0) * (cells[4] - kinetic)], inverse


def rebuild(profile, axis):
    after = shifted(profile, 1, axis)
    edge = 7.0 / 12.0 * (profile + after) - 1.0 / 12.0 * (
        shifted(profile, -1, axis) + shifted(profile, 2, axis)
    )
    edge = jnp.clip(edge, jnp.minimum(profile, after), jnp.maximum(profile, after))
    rise = edge - profile
    fall = profile - shifted(edge, -1, axis)
    right = profile + minmod(rise, 2.0 * fall)
    left = profile - minmod(fall, 2.0 * rise)
    return right, shifted(left, 1, axis)


def face_terms(state, normal):
    density, pressure = state[0], state[4]
    speed = state[normal]
    momentum = [density * state[k] for k in (1, 2, 3)]
    square = state[1] * momentum[0] + state[2] * momentum[1] + state[3] * momentum[2]
    energy = pressure * (1.0 / (GAMMA - 1.0)) + 0.5 * square
    conserved = [density, *momentum, energy]
    flux = [momentum[normal - 1]]
    for k in range(3):
        term = speed * momentum[k]
        flux.append(term + pressure if k == normal - 1 else term)
    flux.append(speed * (energy + pressure))
    return conserved, flux, jnp.abs(speed) + jnp.sqrt(GAMMA * pressure / density)


def flux_difference(cells, axis, normal):
    states, _ = primitives(cells)
    faces = [rebuild(profile, axis) for profile in states]
    left = face_terms([pair[0] for pair in faces], normal)
    right = face_terms([pair[1] for pair in faces], normal)
    signal = 0.5 * jnp.maximum(left[2], right[2])
    differences = []
    for k in range(FIELDS):
        flux = 0.5 * (left[1][k] + right[1][k]) - signal * (right[0][k] - left[0][k])
        differences.append(flux - shifted(flux, -1, axis))
    return differences


def start_kernel(fields_ref, peak_ref, first_ref, last_ref):
    rows = fields_ref.shape[1]
    for k in range(FIELDS):
        first_ref[k * WIDTH : (k + 1) * WIDTH, :] = fields_ref[k, :WIDTH, :]
        last_ref[k * WIDTH : (k + 1) * WIDTH, :] = fields_ref[k, rows - WIDTH :, :]
    first_ref[FIELDS * WIDTH :, :] = fields_ref[0, :1, :]
    last_ref[FIELDS * WIDTH :, :] = fields_ref[0, :1, :]
    (density, *velocity, pressure), _ = primitives([fields_ref[k] for k in range(FIELDS)])
    speed = jnp.maximum(jnp.abs(velocity[0]), jnp.abs(velocity[1]))
    speed = speed + jnp.sqrt(GAMMA * pressure / density)
    peak = jnp.max(speed, axis=0, keepdims=True)
    peak_ref[...] = jnp.broadcast_to(peak[None], peak_ref.shape)


def extended_rows(fields_ref, before_ref, after_ref, full_ref):
    rows = fields_ref.shape[1]
    for k in range(FIELDS):
        full_ref[k, :rows, :] = fields_ref[k]
        full_ref[k, rows : rows + 8, :] = fields_ref[k, :8, :]
        full_ref[k, rows : rows + WIDTH, :] = after_ref[k * WIDTH : (k + 1) * WIDTH, :]
        full_ref[k, rows + 8 - WIDTH : rows + 8, :] = before_ref[k * WIDTH : (k + 1) * WIDTH, :]


def side_kernel(me_ref, fields_ref, peaks_ref, before_ref, after_ref, send_ref, full_ref):
    count = send_ref.shape[0]
    rows, columns = fields_ref.shape[1:]
    extended_rows(fields_ref, before_ref, after_ref, full_ref)
    peak = jnp.max(peaks_ref[...], axis=0)
    lane = lax.broadcasted_iota(jnp.int32, (rows + 8, columns), 1)
    packed = jnp.zeros((rows + 8, columns), jnp.float32)
    for k in range(FIELDS):
        cells = full_ref[k]
        at = k * WIDTH
        ends = pltpu.roll(cells, (at + WIDTH) % columns, 1)
        starts = pltpu.roll(cells, PACKED + at, 1)
        packed = jnp.where((lane >= at) & (lane < at + WIDTH), ends, packed)
        packed = jnp.where((lane >= PACKED + at) & (lane < PACKED + at + WIDTH), starts, packed)
    pad = jnp.zeros((columns - rows - 8, columns), jnp.float32)
    turned = jnp.transpose(jnp.concatenate([packed, pad], axis=0))
    bottom = lax.broadcasted_iota(jnp.int32, (PACKED, columns), 0) == PACKED - 1
    ends = jnp.where(bottom, peak, turned[:PACKED])
    starts = jnp.where(bottom, peak, turned[PACKED : 2 * PACKED])
    for j in range(count):
        send_ref[j] = ends
    me = me_ref[0]
    send_ref[lax.rem(me + count - 1, count)] = starts


def sweep_kernel(me_ref, fields_ref, before_ref, after_ref, received_ref, out_ref, full_ref, half_ref):
    count = received_ref.shape[0]
    rows, columns = fields_ref.shape[1:]
    me = me_ref[0]
    peak = jnp.max(received_ref[...], axis=0)[PACKED - 1 :, :]
    time_step = COURANT / jnp.max(peak, axis=1, keepdims=True)
    extended_rows(fields_ref, before_ref, after_ref, full_ref)
    left = received_ref[lax.rem(me + count - 1, count)]
    right = received_ref[lax.rem(me + 1, count)]
    pad = jnp.zeros((columns - 2 * PACKED, columns), jnp.float32)
    turned = jnp.transpose(jnp.concatenate([right, left, pad], axis=0))
    step = jnp.broadcast_to(time_step, (8, columns))
    lane = lax.broadcasted_iota(jnp.int32, (8, columns), 1)
    for row in range(0, rows + 8, 8):
        strip = turned[row : row + 8]
        own = [full_ref[k, row : row + 8, :] for k in range(FIELDS)]
        cells = []
        for k in range(FIELDS):
            after = pltpu.roll(strip, (-k * WIDTH) % columns, 1)
            before = pltpu.roll(strip, (columns - WIDTH - PACKED - k * WIDTH) % columns, 1)
            side = jnp.where(lane < WIDTH, after, jnp.where(lane >= columns - WIDTH, before, own[k]))
            cells.append(jnp.concatenate([own[k], side], axis=1))
        change = flux_difference(cells, 1, 1)
        for k in range(FIELDS):
            half_ref[k, row : row + 8, :] = own[k] - step * change[k][:, :columns]
    cells = [half_ref[k] for k in range(FIELDS)]
    change = flux_difference(cells, 0, 2)
    for k in range(FIELDS):
        out_ref[k] = (cells[k] - time_step * change[k])[:rows]


def call(kernel, out_shape, n_smem, n_vmem, scratch=()):
    return pl.pallas_call(
        kernel,
        out_shape=out_shape,
        in_specs=[SMEM] * n_smem + [VMEM] * n_vmem,
        out_specs=jax.tree.map(lambda _: VMEM, out_shape),
        scratch_shapes=list(scratch),
    )


def f32(*shape):
    return jax.ShapeDtypeStruct(shape, jnp.float32)


def local(fields):
    rows, columns = fields.shape[2:]
    cells = fields.reshape(FIELDS, rows, columns)
    count_row, count_col = lax.axis_size(ROW), lax.axis_size(COL)
    me = lax.axis_index(ROW).astype(jnp.int32).reshape(1)
    full = pltpu.VMEM((FIELDS, rows + 8, columns), jnp.float32)
    packed = f32(PACKED, columns)

    peaks, first, last = call(start_kernel, (f32(count_col, 1, columns), packed, packed), 0, 1)(cells)
    up = [(i, (i + 1) % count_col) for i in range(count_col)]
    before = lax.ppermute(last, COL, up)
    after = lax.ppermute(first, COL, [(j, i) for i, j in up])
    peaks = lax.all_to_all(peaks, COL, 0, 0, tiled=True)
    send = call(side_kernel, f32(count_row, PACKED, columns), 1, 4, [full])(me, cells, peaks, before, after)
    received = lax.all_to_all(send, ROW, 0, 0, tiled=True)
    out = call(sweep_kernel, f32(FIELDS, rows, columns), 1, 4, [full, full])(
        me, cells, before, after, received
    )
    return out.reshape(fields.shape)


def solution(mesh):
    split = Mesh(mesh.devices.reshape(8, 2, 8, 4, 2), (*ROW, *COL))
    placed = (P(None, None, COL, ROW),)
    return jax.shard_map(
        local, mesh=split, in_specs=placed, out_specs=P(None, None, COL, ROW), check_vma=False
    )
```

time: 94.2 us -> 61.4 us (0.65); the launches traced: 92.8 us -> 61 us
  blocking collectives: 65.7 us -> 17.8 us
  starting transfers between devices: 15.7 us -> 29.2 us
  Pallas kernels: 0 us -> 8.03 us
  other arithmetic: 4.75 us -> 0 us
  waiting for transfers between devices: 3.77 us -> 5.31 us
  local copies, waits for them, and re-layouts: 1.87 us -> 0.62 us
  between operations: 1.03 us -> 0.07 us
    pmax x5 -> x0, blocking collectives: 65.7 us -> none  [one_axis_at_a_time(): shard = lax.pmax(shard, axis)]
    all_to_all x0 -> x1, starting transfers between devices: none -> 22.9 us  [local(): peaks = lax.all_to_all(peaks, COL, 0, 0, tiled=True)]
    all_to_all x0 -> x1, blocking collectives: none -> 17.8 us  [local(): received = lax.all_to_all(send, ROW, 0, 0, tiled=True)]
    ppermute x4 -> x2, starting transfers between devices: 15.7 us -> 6.36 us  [the longest x1 4.44 us: local(): before = lax.ppermute(last, COL, up)]
    pallas_call x0 -> x3, Pallas kernels: none -> 8.03 us  [the longest x1 4.61 us: local(): call(sweep_kernel, f32(FIELDS, rows, columns), 1, 4, [full, full])]
    sub x12 -> x0, other arithmetic: 2.01 us -> none  [the longest x4 1.57 us: sweep_along(): 0.5 * (left_flux[component] + right_flux[component])]
    slice x2 -> x0, local copies, waits for them, and re-layouts: 1.17 us -> none  [extended(): last = lax.slice_in_dim(shard, length - width, length, axis=dim)]
    all_to_all x0 -> x1, waiting for transfers between devices: none -> 1.1 us  [local(): peaks = lax.all_to_all(peaks, COL, 0, 0, tiled=True)]
  transfers between devices with their start and end apart: 4 -> 3, of which waited for: 1 -> 2; matrix products, arithmetic and copies ran while one was open for 1% -> 0% of each run, Pallas kernels for 0% -> 0%
where the time goes in v1:
time: 61.4 us; the launch traced here: 61 us
  starting transfers between devices  29.2 us (48%)
  blocking collectives  17.8 us (29%)
  Pallas kernels  8.03 us (13%)
  waiting for transfers between devices  5.31 us (9%)
  local copies, waits for them, and re-layouts  0.62 us (1%)
    all_to_all x1, starting transfers between devices, local(): peaks = lax.all_to_all(peaks, COL, 0, 0, tiled=True)  22.9 us
    all_to_all x1, blocking collectives, local(): received = lax.all_to_all(send, ROW, 0, 0, tiled=True)  17.8 us
    pallas_call x1, Pallas kernels, local(): call(sweep_kernel, f32(FIELDS, rows, columns), 1, 4, [full, full])  4.61 us
    ppermute x1, starting transfers between devices, local(): before = lax.ppermute(last, COL, up)  4.44 us
    ppermute x1, waiting for transfers between devices, local(): after = lax.ppermute(first, COL, [(j, i) for i, j in up])  4.21 us
    ppermute x1, starting transfers between devices, local(): after = lax.ppermute(first, COL, [(j, i) for i, j in up])  1.92 us
    pallas_call x1, Pallas kernels, local(): call(side_kernel, f32(count_row, PACKED, columns), 1, 4, [full])  1.82 us
    pallas_call x1, Pallas kernels, local(): call(start_kernel, (f32(count_col, 1, columns), packed, packed), 0, 1)  1.59 us
  transfers between devices with their start and end apart: 3, of which 2 were waited for; matrix products, arithmetic and copies ran while one was open for 0% of the time, Pallas kernels for 0%

profile of v1, /device:TPU:1, one launch (start us, length us, event | category | flops | bytes accessed | tf_op | source)
XLA Modules:
  0.0 61.0 jit_solution(235980403626376300)
XLA Ops:
  0.0 1.6 %shard_map.17 = (f32[64,1,128]{2,1,0:T(1,128)}, f32[16,128]{1,0:T(8,128)}, f32[16,128]{1,0:T(8,128)}) custom-call(f32[5,64,128]{2,1,0:T(8,128)} %bitcast.5), custom_call_target="tpu_custom_call" | custom-call | tf_op jit(solution)/shard_map/pallas_call | solution.py:180
  1.6 0.0 copy-start.4
  1.6 0.0 copy-start.3
  1.6 22.9 %all-to-all-start = ((f32[64,1,128]{2,1,0:T(1,128)}), f32[64,1,128]{2,1,0:T(1,128)S(1)}, u32[]{:S(2)}, u32[]{:S(2)}) async-start(f32[64,1,128]{2,1,0:T(1,128)} %get-tuple-element.10), calls=%async_computation | async-start | bytes 65536 | tf_op jit(solution)/shard_map/all_to_all | solution.py:184
  24.5 0.0 copy-done.4
  24.5 4.4 %collective-permute-start = (f32[16,128]{1,0:T(8,128)S(1)}, f32[16,128]{1,0:T(8,128)S(1)}, u32[]{:S(2)}, u32[]{:S(2)}) collective-permute-start(f32[16,128]{1,0:T(8,128)S(1)} %copy-done.4), channel_id=1, source_target_pairs={{0,1},{1,2},{2,3},{3,4},{4,5},{5,6},{6,7},{7,8},{8,9},{9,10},{10,1... | collective-permute-start | bytes 24584 | tf_op jit(solution)/shard_map/ppermute | solution.py:182
  28.9 0.0 copy-done.3
  28.9 1.9 %collective-permute-start.1 = (f32[16,128]{1,0:T(8,128)S(1)}, f32[16,128]{1,0:T(8,128)S(1)}, u32[]{:S(2)}, u32[]{:S(2)}) collective-permute-start(f32[16,128]{1,0:T(8,128)S(1)} %copy-done.3), channel_id=1, source_target_pairs={{1,0},{2,1},{3,2},{4,3},{5,4},{6,5},{7,6},{8,7},{9,8},{10,9},{11,1... | collective-permute-start | bytes 24584 | tf_op jit(solution)/shard_map/ppermute | solution.py:183
  30.9 0.0 collective-permute-done.before_ref
  30.9 0.0 copy-start.1
  30.9 4.2 %collective-permute-done.1.after_ref = f32[16,128]{1,0:T(8,128)S(1)} collective-permute-done((f32[16,128]{1,0:T(8,128)S(1)}, f32[16,128]{1,0:T(8,128)S(1)}, u32[]{:S(2)}, u32[]{:S(2)}) %collective-permute-start.1) | collective-permute-done | bytes 8224 | tf_op jit(solution)/shard_map/ppermute | solution.py:183
  35.1 0.0 copy-start.2
  35.1 1.1 %all-to-all-done.peaks_ref = f32[64,1,128]{2,1,0:T(1,128)S(1)} async-done(((f32[64,1,128]{2,1,0:T(1,128)}), f32[64,1,128]{2,1,0:T(1,128)S(1)}, u32[]{:S(2)}, u32[]{:S(2)}) %all-to-all-start) | async-done | bytes 32800 | tf_op jit(solution)/shard_map/all_to_all | solution.py:184
  36.2 0.0 copy-start
  36.2 0.0 copy-done.1
  36.2 0.0 copy-done.2
  36.2 0.6 copy-done
  36.8 1.8 %shard_map.18 = f32[16,16,128]{2,1,0:T(8,128)} custom-call(s32[1]{0:T(128)} %bitcast.me_ref, f32[5,64,128]{2,1,0:T(8,128)} %bitcast.6, f32[64,1,128]{2,1,0:T(1,128)} %copy-done, f32[16,128]{1,0:T(8,128)} %copy-done.1, f32[16,128]{1,0:T(8,128)} %copy-done.2), custom_call_target="tpu_custom_call" | custom-call | tf_op jit(solution)/shard_map/pallas_call | solution.py:185
  38.6 17.8 %all_to_all.10.received_ref = f32[16,16,128]{2,1,0:T(8,128)} all-to-all(f32[16,16,128]{2,1,0:T(8,128)} %shard_map.18), channel_id=1, replica_groups=mesh['row_0'=8,'row_1'=2,'col_0'=8,'col_1'=4,'col_2'=2] {'row_0','row_1'}, dimensions={0} | all-to-all | bytes 262144 | tf_op jit(solution)/shard_map/all_to_all | solution.py:186
  56.4 4.6 %shard_map.19 = f32[5,64,128]{2,1,0:T(8,128)} custom-call(s32[1]{0:T(128)} %bitcast.me_ref, f32[5,64,128]{2,1,0:T(8,128)} %bitcast.7, f32[16,128]{1,0:T(8,128)} %copy-done.1, f32[16,128]{1,0:T(8,128)} %copy-done.2, f32[16,16,128]{2,1,0:T(8,128)} %all_to_all.10.received_ref), custom_call_target="tpu_custom_call" | custom-call | tf_op jit(solution)/shard_map/pallas_call | solution.py:187
Async XLA Ops:
  1.6 22.9 %copy-start.4 = (f32[16,128]{1,0:T(8,128)S(1)}, f32[16,128]{1,0:T(8,128)}, u32[]{:S(2)}) copy-start(f32[16,128]{1,0:T(8,128)} %get-tuple-element.8) | copy-start | bytes 24580
  1.6 27.3 %copy-start.3 = (f32[16,128]{1,0:T(8,128)S(1)}, f32[16,128]{1,0:T(8,128)}, u32[]{:S(2)}) copy-start(f32[16,128]{1,0:T(8,128)} %get-tuple-element.9) | copy-start | bytes 24580
  1.6 34.6 %all-to-all-start = ((f32[64,1,128]{2,1,0:T(1,128)}), f32[64,1,128]{2,1,0:T(1,128)S(1)}, u32[]{:S(2)}, u32[]{:S(2)}) async-start(f32[64,1,128]{2,1,0:T(1,128)} %get-tuple-element.10), calls=%async_computation | async-start | bytes 65536 | tf_op jit(solution)/shard_map/all_to_all | solution.py:184
  24.5 6.4 %collective-permute-start = (f32[16,128]{1,0:T(8,128)S(1)}, f32[16,128]{1,0:T(8,128)S(1)}, u32[]{:S(2)}, u32[]{:S(2)}) collective-permute-start(f32[16,128]{1,0:T(8,128)S(1)} %copy-done.4), channel_id=1, source_target_pairs={{0,1},{1,2},{2,3},{3,4},{4,5},{5,6},{6,7},{7,8},{8,9},{9,10},{10,1... | collective-permute-start | bytes 24584 | tf_op jit(solution)/shard_map/ppermute | solution.py:182
  28.9 6.2 %collective-permute-start.1 = (f32[16,128]{1,0:T(8,128)S(1)}, f32[16,128]{1,0:T(8,128)S(1)}, u32[]{:S(2)}, u32[]{:S(2)}) collective-permute-start(f32[16,128]{1,0:T(8,128)S(1)} %copy-done.3), channel_id=1, source_target_pairs={{1,0},{2,1},{3,2},{4,3},{5,4},{6,5},{7,6},{8,7},{9,8},{10,9},{11,1... | collective-permute-start | bytes 24584 | tf_op jit(solution)/shard_map/ppermute | solution.py:183
  30.9 5.3 %copy-start.1 = (f32[16,128]{1,0:T(8,128)}, f32[16,128]{1,0:T(8,128)S(1)}, u32[]{:S(2)}) copy-start(f32[16,128]{1,0:T(8,128)S(1)} %collective-permute-done.before_ref) | copy-start | bytes 24580
  35.1 1.1 %copy-start.2 = (f32[16,128]{1,0:T(8,128)}, f32[16,128]{1,0:T(8,128)S(1)}, u32[]{:S(2)}) copy-start(f32[16,128]{1,0:T(8,128)S(1)} %collective-permute-done.1.after_ref) | copy-start | bytes 24580
  36.2 0.6 copy-start

commit v2 on v1

--- a/solution.py
+++ b/solution.py
@@ -99,57 +99,67 @@
         full_ref[k, rows + 8 - WIDTH : rows + 8, :] = before_ref[k * WIDTH : (k + 1) * WIDTH, :]
 
 
-def side_kernel(me_ref, fields_ref, peaks_ref, before_ref, after_ref, send_ref, full_ref):
-    count = send_ref.shape[0]
+def pack_kernel(fields_ref, before_ref, after_ref, full_ref, own_ref):
     rows, columns = fields_ref.shape[1:]
     extended_rows(fields_ref, before_ref, after_ref, full_ref)
-    peak = jnp.max(peaks_ref[...], axis=0)
     lane = lax.broadcasted_iota(jnp.int32, (rows + 8, columns), 1)
     packed = jnp.zeros((rows + 8, columns), jnp.float32)
     for k in range(FIELDS):
-        cells = full_ref[k]
-        at = k * WIDTH
-        ends = pltpu.roll(cells, (at + WIDTH) % columns, 1)
-        starts = pltpu.roll(cells, PACKED + at, 1)
-        packed = jnp.where((lane >= at) & (lane < at + WIDTH), ends, packed)
-        packed = jnp.where((lane >= PACKED + at) & (lane < PACKED + at + WIDTH), starts, packed)
+        at = k * 4 * WIDTH
+        ends = pltpu.roll(full_ref[k], at + 2 * WIDTH, 1)
+        packed = jnp.where((lane >= at) & (lane < at + 4 * WIDTH), ends, packed)
     pad = jnp.zeros((columns - rows - 8, columns), jnp.float32)
-    turned = jnp.transpose(jnp.concatenate([packed, pad], axis=0))
-    bottom = lax.broadcasted_iota(jnp.int32, (PACKED, columns), 0) == PACKED - 1
-    ends = jnp.where(bottom, peak, turned[:PACKED])
-    starts = jnp.where(bottom, peak, turned[PACKED : 2 * PACKED])
+    own_ref[...] = jnp.transpose(jnp.concatenate([packed, pad], axis=0))[: own_ref.shape[0]]
+
+
+def fill_kernel(me_ref, peaks_ref, own_ref, send_ref):
+    count = send_ref.shape[0]
+    before = lax.rem(me_ref[0] + count - 1, count)
+    peak = jnp.max(peaks_ref[...], axis=0)
     for j in range(count):
-        send_ref[j] = ends
+        send_ref[j, PACKED - 1 :, :] = peak
+        for k in range(FIELDS):
+            at = k * 4 * WIDTH + WIDTH
+            send_ref[j, k * WIDTH : (k + 1) * WIDTH, :] = own_ref[at : at + WIDTH, :]
+    for k in range(FIELDS):
+        at = k * 4 * WIDTH + 2 * WIDTH
+        send_ref[before, k * WIDTH : (k + 1) * WIDTH, :] = own_ref[at : at + WIDTH, :]
+
+
+def inner_kernel(full_ref, change_ref):
+    for row in range(0, full_ref.shape[1], 8):
+        change = flux_difference([full_ref[k, row : row + 8, :] for k in range(FIELDS)], 1, 1)
+        for k in range(FIELDS):
+            change_ref[k, row : row + 8, :] = change[k]
+
+
+def sweep_kernel(me_ref, full_ref, change_ref, own_ref, received_ref, out_ref, strip_ref, turned_ref):
+    count = received_ref.shape[0]
+    rows, columns = out_ref.shape[1:]
     me = me_ref[0]
-    send_ref[lax.rem(me + count - 1, count)] = starts
-
-
-def sweep_kernel(me_ref, fields_ref, before_ref, after_ref, received_ref, out_ref, full_ref, half_ref):
-    count = received_ref.shape[0]
-    rows, columns = fields_ref.shape[1:]
-    me = me_ref[0]
-    peak = jnp.max(received_ref[...], axis=0)[PACKED - 1 :, :]
+    before, after = lax.rem(me + count - 1, count), lax.rem(me + 1, count)
+    peak = jnp.max(received_ref[:, PACKED - 1, :], axis=0, keepdims=True)
     time_step = COURANT / jnp.max(peak, axis=1, keepdims=True)
-    extended_rows(fields_ref, before_ref, after_ref, full_ref)
-    left = received_ref[lax.rem(me + count - 1, count)]
-    right = received_ref[lax.rem(me + 1, count)]
-    pad = jnp.zeros((columns - 2 * PACKED, columns), jnp.float32)
-    turned = jnp.transpose(jnp.concatenate([right, left, pad], axis=0))
-    step = jnp.broadcast_to(time_step, (8, columns))
-    lane = lax.broadcasted_iota(jnp.int32, (8, columns), 1)
-    for row in range(0, rows + 8, 8):
-        strip = turned[row : row + 8]
-        own = [full_ref[k, row : row + 8, :] for k in range(FIELDS)]
-        cells = []
-        for k in range(FIELDS):
-            after = pltpu.roll(strip, (-k * WIDTH) % columns, 1)
-            before = pltpu.roll(strip, (columns - WIDTH - PACKED - k * WIDTH) % columns, 1)
-            side = jnp.where(lane < WIDTH, after, jnp.where(lane >= columns - WIDTH, before, own[k]))
-            cells.append(jnp.concatenate([own[k], side], axis=1))
-        change = flux_difference(cells, 1, 1)
-        for k in range(FIELDS):
-            half_ref[k, row : row + 8, :] = own[k] - step * change[k][:, :columns]
-    cells = [half_ref[k] for k in range(FIELDS)]
+    for k in range(FIELDS):
+        at, own = k * WIDTH, k * 4 * WIDTH
+        strip_ref[k, :6, :] = own_ref[own : own + 6, :]
+        strip_ref[k, 6:9, :] = received_ref[after, at : at + WIDTH, :]
+        strip_ref[k, 9:12, :] = received_ref[before, at : at + WIDTH, :]
+        strip_ref[k, 12:18, :] = own_ref[own + 6 : own + 12, :]
+        strip_ref[k, 18:, :] = own_ref[own : own + 6, :]
+    edge = flux_difference([strip_ref[k] for k in range(FIELDS)], 0, 1)
+    turned_ref[...] = jnp.zeros_like(turned_ref)
+    for k in range(FIELDS):
+        turned_ref[6 * k : 6 * k + 3, :] = edge[k][3:6]
+        turned_ref[6 * k + 3 : 6 * k + 6, :] = edge[k][12:15]
+    turned = jnp.transpose(turned_ref[...])[: rows + 8]
+    lane = lax.broadcasted_iota(jnp.int32, (rows + 8, columns), 1)
+    at_edge = (lane < WIDTH) | (lane >= columns - WIDTH)
+    cells = []
+    for k in range(FIELDS):
+        sides = pltpu.roll(turned, columns - WIDTH - 6 * k, 1)
+        change = jnp.where(at_edge, sides, change_ref[k])
+        cells.append(full_ref[k] - time_step * change)
     change = flux_difference(cells, 0, 2)
     for k in range(FIELDS):
         out_ref[k] = (cells[k] - time_step * change[k])[:rows]
@@ -162,11 +172,20 @@
         in_specs=[SMEM] * n_smem + [VMEM] * n_vmem,
         out_specs=jax.tree.map(lambda _: VMEM, out_shape),
         scratch_shapes=list(scratch),
+        cost_estimate=pl.CostEstimate(flops=4_000_000, bytes_accessed=1_000_000, transcendentals=0),
     )
 
 
 def f32(*shape):
     return jax.ShapeDtypeStruct(shape, jnp.float32)
+
+
+def kept(*shape):
+    return pltpu.VMEM(shape, jnp.float32)
+
+
+def held(*arrays):
+    return [pltpu.with_memory_space_constraint(array, pltpu.VMEM) for array in arrays]
 
 
 def local(fields):
@@ -174,18 +193,23 @@
     cells = fields.reshape(FIELDS, rows, columns)
     count_row, count_col = lax.axis_size(ROW), lax.axis_size(COL)
     me = lax.axis_index(ROW).astype(jnp.int32).reshape(1)
-    full = pltpu.VMEM((FIELDS, rows + 8, columns), jnp.float32)
-    packed = f32(PACKED, columns)
-
-    peaks, first, last = call(start_kernel, (f32(count_col, 1, columns), packed, packed), 0, 1)(cells)
+    full = (FIELDS, rows + 8, columns)
+    packed = kept(PACKED, columns)
+    own = kept(64, columns)
     up = [(i, (i + 1) % count_col) for i in range(count_col)]
+
+    shapes = (kept(count_col, 1, columns), packed, packed)
+    peaks, first, last = call(start_kernel, shapes, 0, 1)(cells)
     before = lax.ppermute(last, COL, up)
     after = lax.ppermute(first, COL, [(j, i) for i, j in up])
     peaks = lax.all_to_all(peaks, COL, 0, 0, tiled=True)
-    send = call(side_kernel, f32(count_row, PACKED, columns), 1, 4, [full])(me, cells, peaks, before, after)
+    grown, own = call(pack_kernel, (kept(*full), own), 0, 3)(cells, *held(before, after))
+    send = call(fill_kernel, kept(count_row, PACKED, columns), 1, 2)(me, *held(peaks, own))
     received = lax.all_to_all(send, ROW, 0, 0, tiled=True)
-    out = call(sweep_kernel, f32(FIELDS, rows, columns), 1, 4, [full, full])(
-        me, cells, before, after, received
+    change = call(inner_kernel, kept(*full), 0, 1)(*held(grown))
+    scratch = [pltpu.VMEM((FIELDS, 24, columns), jnp.float32), pltpu.VMEM((columns, columns), jnp.float32)]
+    out = call(sweep_kernel, f32(FIELDS, rows, columns), 1, 4, scratch)(
+        me, *held(grown, change, own, received)
     )
     return out.reshape(fields.shape)
 

time: 61.4 us -> 57.1 us (0.930)
  the two profiles are of different devices: /device:TPU:1 before, /device:TPU:8 now
where the time goes in v2:
time: 57.1 us; the launch traced here: 56.8 us
  starting transfers between devices  41 us (72%)
  waiting for transfers between devices  10.4 us (18%)
  Pallas kernels  5.3 us (9%)
    all_to_all x1, starting transfers between devices, local(): peaks = lax.all_to_all(peaks, COL, 0, 0, tiled=True)  21.8 us
    all_to_all x1, starting transfers between devices, local(): received = lax.all_to_all(send, ROW, 0, 0, tiled=True)  9.48 us
    all_to_all x1, waiting for transfers between devices, local(): received = lax.all_to_all(send, ROW, 0, 0, tiled=True)  9.06 us
    ppermute x1, starting transfers between devices, local(): after = lax.ppermute(first, COL, [(j, i) for i, j in up])  7.75 us
    ppermute x1, starting transfers between devices, local(): before = lax.ppermute(last, COL, up)  2.03 us
    pallas_call x1, Pallas kernels, local(): peaks, first, last = call(start_kernel, shapes, 0, 1)(cells)  1.59 us
    pallas_call x1, Pallas kernels, local(): call(sweep_kernel, f32(FIELDS, rows, columns), 1, 4, scratch)  1.36 us
    ppermute x1, waiting for transfers between devices, local(): after = lax.ppermute(first, COL, [(j, i) for i, j in up])  1.33 us
  transfers between devices with their start and end apart: 4, of which 2 were waited for; matrix products, arithmetic and copies ran while one was open for 0% of the time, Pallas kernels for 3%

profile of v2, /device:TPU:8, one launch (start us, length us, event | category | flops | bytes accessed | tf_op | source)
XLA Modules:
  0.0 56.8 jit_solution(14387608874620459013)
XLA Ops:
  0.0 1.6 %shard_map.17 = (f32[64,1,128]{2,1,0:T(1,128)}, f32[16,128]{1,0:T(8,128)S(1)}, f32[16,128]{1,0:T(8,128)S(1)}) custom-call(f32[5,64,128]{2,1,0:T(8,128)} %bitcast.5), custom_call_target="tpu_custom_call" | custom-call | flops 4000000 | bytes 1000000 | tf_op jit(solution)/shard_map/pallas_call | solution.py:202
  1.6 21.8 %all-to-all-start = ((f32[64,1,128]{2,1,0:T(1,128)}), f32[64,1,128]{2,1,0:T(1,128)S(1)}, u32[]{:S(2)}, u32[]{:S(2)}) async-start(f32[64,1,128]{2,1,0:T(1,128)} %get-tuple-element.14), calls=%async_computation | async-start | bytes 65536 | tf_op jit(solution)/shard_map/all_to_all | solution.py:205
  23.4 2.0 %collective-permute-start = (f32[16,128]{1,0:T(8,128)S(1)}, f32[16,128]{1,0:T(8,128)S(1)}, u32[]{:S(2)}, u32[]{:S(2)}) collective-permute-start(f32[16,128]{1,0:T(8,128)S(1)} %get-tuple-element.10), channel_id=1, source_target_pairs={{0,1},{1,2},{2,3},{3,4},{4,5},{5,6},{6,7},{7,8},{8,9},{9,10},{10,1... | collective-permute-start | bytes 24584 | tf_op jit(solution)/shard_map/ppermute | solution.py:203
  25.4 7.8 %collective-permute-start.1 = (f32[16,128]{1,0:T(8,128)S(1)}, f32[16,128]{1,0:T(8,128)S(1)}, u32[]{:S(2)}, u32[]{:S(2)}) collective-permute-start(f32[16,128]{1,0:T(8,128)S(1)} %get-tuple-element.11), channel_id=1, source_target_pairs={{1,0},{2,1},{3,2},{4,3},{5,4},{6,5},{7,6},{8,7},{9,8},{10,9},{11,1... | collective-permute-start | bytes 24584 | tf_op jit(solution)/shard_map/ppermute | solution.py:204
  33.2 0.0 collective-permute-done.before_ref
  33.2 1.3 %collective-permute-done.1.after_ref = f32[16,128]{1,0:T(8,128)S(1)} collective-permute-done((f32[16,128]{1,0:T(8,128)S(1)}, f32[16,128]{1,0:T(8,128)S(1)}, u32[]{:S(2)}, u32[]{:S(2)}) %collective-permute-start.1) | collective-permute-done | bytes 8224 | tf_op jit(solution)/shard_map/ppermute | solution.py:204
  34.5 1.1 %shard_map.18 = (f32[5,72,128]{2,1,0:T(8,128)S(1)}, f32[64,128]{1,0:T(8,128)S(1)}) custom-call(f32[5,64,128]{2,1,0:T(8,128)} %bitcast.6, f32[16,128]{1,0:T(8,128)S(1)} %collective-permute-done.before_ref, f32[16,128]{1,0:T(8,128)S(1)} %collective-permute-done.1.after_ref), custom_call_target="tpu_custom_call" | custom-call | flops 4000000 | bytes 1000000 | tf_op jit(solution)/shard_map/pallas_call | solution.py:206
  35.6 0.0 all-to-all-done.peaks_ref
  35.6 0.7 %shard_map.20 = f32[16,16,128]{2,1,0:T(8,128)} custom-call(s32[1]{0:T(128)} %bitcast.me_ref, f32[64,1,128]{2,1,0:T(1,128)S(1)} %all-to-all-done.peaks_ref, f32[64,128]{1,0:T(8,128)S(1)} %get-tuple-element.13.own_ref), custom_call_target="tpu_custom_call" | custom-call | flops 4000000 | bytes 1000000 | tf_op jit(solution)/shard_map/pallas_call | solution.py:207
  36.3 9.5 %all-to-all-start.1 = ((f32[16,16,128]{2,1,0:T(8,128)}), f32[16,16,128]{2,1,0:T(8,128)S(1)}, u32[]{:S(2)}, u32[]{:S(2)}) async-start(f32[16,16,128]{2,1,0:T(8,128)} %shard_map.20), calls=%async_computation.1 | async-start | bytes 262144 | tf_op jit(solution)/shard_map/all_to_all | solution.py:208
  45.8 0.6 shard_map.19.change_ref
  46.4 9.1 %all-to-all-done.1.received_ref = f32[16,16,128]{2,1,0:T(8,128)S(1)} async-done(((f32[16,16,128]{2,1,0:T(8,128)}), f32[16,16,128]{2,1,0:T(8,128)S(1)}, u32[]{:S(2)}, u32[]{:S(2)}) %all-to-all-start.1) | async-done | bytes 131104 | tf_op jit(solution)/shard_map/all_to_all | solution.py:208
  55.4 1.4 %shard_map.21 = f32[5,64,128]{2,1,0:T(8,128)} custom-call(s32[1]{0:T(128)} %bitcast.me_ref, f32[5,72,128]{2,1,0:T(8,128)S(1)} %get-tuple-element.12.full_ref, f32[5,72,128]{2,1,0:T(8,128)S(1)} %shard_map.19.change_ref, f32[64,128]{1,0:T(8,128)S(1)} %get-tuple-element.13.own_ref, f32[16,16,128]{2,1,0:T(8,128)S(1)} %all-to-all-done.1.received_ref), custom_call_target="tpu_custom_call" | custom-call | flops 4000000 | bytes 1000000 | tf_op jit(solution)/shard_map/pallas_call | solution.py:211
Async XLA Ops:
  1.6 34.0 %all-to-all-start = ((f32[64,1,128]{2,1,0:T(1,128)}), f32[64,1,128]{2,1,0:T(1,128)S(1)}, u32[]{:S(2)}, u32[]{:S(2)}) async-start(f32[64,1,128]{2,1,0:T(1,128)} %get-tuple-element.14), calls=%async_computation | async-start | bytes 65536 | tf_op jit(solution)/shard_map/all_to_all | solution.py:205
  23.4 9.8 %collective-permute-start = (f32[16,128]{1,0:T(8,128)S(1)}, f32[16,128]{1,0:T(8,128)S(1)}, u32[]{:S(2)}, u32[]{:S(2)}) collective-permute-start(f32[16,128]{1,0:T(8,128)S(1)} %get-tuple-element.10), channel_id=1, source_target_pairs={{0,1},{1,2},{2,3},{3,4},{4,5},{5,6},{6,7},{7,8},{8,9},{9,10},{10,1... | collective-permute-start | bytes 24584 | tf_op jit(solution)/shard_map/ppermute | solution.py:203
  25.4 9.1 %collective-permute-start.1 = (f32[16,128]{1,0:T(8,128)S(1)}, f32[16,128]{1,0:T(8,128)S(1)}, u32[]{:S(2)}, u32[]{:S(2)}) collective-permute-start(f32[16,128]{1,0:T(8,128)S(1)} %get-tuple-element.11), channel_id=1, source_target_pairs={{1,0},{2,1},{3,2},{4,3},{5,4},{6,5},{7,6},{8,7},{9,8},{10,9},{11,1... | collective-permute-start | bytes 24584 | tf_op jit(solution)/shard_map/ppermute | solution.py:204
  36.3 19.1 %all-to-all-start.1 = ((f32[16,16,128]{2,1,0:T(8,128)}), f32[16,16,128]{2,1,0:T(8,128)S(1)}, u32[]{:S(2)}, u32[]{:S(2)}) async-start(f32[16,16,128]{2,1,0:T(8,128)} %shard_map.20), calls=%async_computation.1 | async-start | bytes 262144 | tf_op jit(solution)/shard_map/all_to_all | solution.py:208

commit v3 on v2

v3 whole, which is shorter than its diff:
```python
import jax
import jax.numpy as jnp
from jax import lax
from jax.experimental import pallas as pl
from jax.experimental.pallas import tpu as pltpu
from jax.sharding import Mesh
from jax.sharding import PartitionSpec as P

ROW = ("row_0", "row_1")
COL = ("col_0", "col_1", "col_2")

GAMMA = 1.4
COURANT = 0.3
WIDTH = 3
FIELDS = 5
PACKED = 8
STRIP = 9
VMEM = pl.BlockSpec(memory_space=pltpu.VMEM)
SMEM = pl.BlockSpec(memory_space=pltpu.SMEM)


def minmod(first, second):
    low = jnp.minimum(first, second)
    high = jnp.maximum(first, second)
    return jnp.maximum(low, 0.0) + jnp.minimum(high, 0.0)


def shifted(profile, step, axis):
    return pltpu.roll(profile, (-step) % profile.shape[axis], axis)


def primitives(cells):
    inverse = 1.0 / cells[0]
    velocity = [cells[k] * inverse for k in (1, 2, 3)]
    kinetic = 0.5 * (cells[1] * velocity[0] + cells[2] * velocity[1] + cells[3] * velocity[2])
    return [cells[0], *velocity, (GAMMA - 1.0) * (cells[4] - kinetic)], inverse


def rebuild(profile, axis):
    after = shifted(profile, 1, axis)
    edge = 7.0 / 12.0 * (profile + after) - 1.0 / 12.0 * (
        shifted(profile, -1, axis) + shifted(profile, 2, axis)
    )
    edge = jnp.clip(edge, jnp.minimum(profile, after), jnp.maximum(profile, after))
    rise = edge - profile
    fall = profile - shifted(edge, -1, axis)
    right = profile + minmod(rise, 2.0 * fall)
    left = profile - minmod(fall, 2.0 * rise)
    return right, shifted(left, 1, axis)


def face_terms(state, normal):
    density, pressure = state[0], state[4]
    speed = state[normal]
    momentum = [density * state[k] for k in (1, 2, 3)]
    square = state[1] * momentum[0] + state[2] * momentum[1] + state[3] * momentum[2]
    energy = pressure * (1.0 / (GAMMA - 1.0)) + 0.5 * square
    conserved = [density, *momentum, energy]
    flux = [momentum[normal - 1]]
    for k in range(3):
        term = speed * momentum[k]
        flux.append(term + pressure if k == normal - 1 else term)
    flux.append(speed * (energy + pressure))
    return conserved, flux, jnp.abs(speed) + jnp.sqrt(GAMMA * pressure / density)


def flux_difference(cells, axis, normal):
    states, _ = primitives(cells)
    faces = [rebuild(profile, axis) for profile in states]
    left = face_terms([pair[0] for pair in faces], normal)
    right = face_terms([pair[1] for pair in faces], normal)
    signal = 0.5 * jnp.maximum(left[2], right[2])
    differences = []
    for k in range(FIELDS):
        flux = 0.5 * (left[1][k] + right[1][k]) - signal * (right[0][k] - left[0][k])
        differences.append(flux - shifted(flux, -1, axis))
    return differences


def start_kernel(me_ref, fields_ref, send_ref, own_ref, cells_ref, swapped_ref):
    count = send_ref.shape[0]
    rows, columns = fields_ref.shape[1:]
    cells = [fields_ref[k] for k in range(FIELDS)]
    for k in range(FIELDS):
        cells_ref[k] = cells[k]
    (density, *velocity, pressure), _ = primitives(cells)
    speed = jnp.maximum(jnp.abs(velocity[0]), jnp.abs(velocity[1]))
    speed = speed + jnp.sqrt(GAMMA * pressure / density)
    peak = jnp.max(speed, axis=0, keepdims=True)
    peak = jnp.maximum(peak, pltpu.roll(peak, rows, 1))
    lane = lax.broadcasted_iota(jnp.int32, (rows, columns), 1)
    ends = starts = jnp.zeros((rows, columns), jnp.float32)
    for k in range(FIELDS):
        at = k * STRIP
        turned = pltpu.roll(cells[k], at + 2 * WIDTH, 1)
        ends = jnp.where((lane >= at) & (lane < at + 2 * WIDTH), turned, ends)
        turned = pltpu.roll(cells[k], at + WIDTH, 1)
        starts = jnp.where((lane >= at + WIDTH) & (lane < at + STRIP), turned, starts)
    own = jnp.transpose(jnp.concatenate([ends, starts], axis=0))[: own_ref.shape[0]]
    own_ref[...] = own
    swapped_ref[...] = pltpu.roll(own, rows, 1)
    half = lax.broadcasted_iota(jnp.int32, (1, columns), 1) < rows

    def row_of(ref, slot):
        at = slot // WIDTH * STRIP + WIDTH + slot % WIDTH
        return ref[at : at + 1, :]

    ends, starts = [], []
    for row in range(PACKED):
        last = row == PACKED - 1
        ends.append(
            jnp.where(half, row_of(own_ref, row), peak if last else row_of(swapped_ref, PACKED + row))
        )
        starts.append(
            jnp.where(half, row_of(swapped_ref, row), peak if last else row_of(own_ref, PACKED + row))
        )
    ends, starts = jnp.concatenate(ends, axis=0), jnp.concatenate(starts, axis=0)
    for j in range(count):
        send_ref[j] = ends
    send_ref[lax.rem(me_ref[0] + count - 1, count)] = starts


def inner_kernel(cells_ref, change_ref):
    for row in range(0, cells_ref.shape[1], 8):
        change = flux_difference([cells_ref[k, row : row + 8, :] for k in range(FIELDS)], 1, 1)
        for k in range(FIELDS):
            change_ref[k, row : row + 8, :] = change[k]


def edge_kernel(
    me_ref, cells_ref, inner_ref, own_ref, received_ref,
    change_ref, first_ref, last_ref, peak_ref, strip_ref, side_ref, turned_ref,
):
    count = received_ref.shape[0]
    rows, columns = cells_ref.shape[1:]
    me = me_ref[0]
    before, after = lax.rem(me + count - 1, count), lax.rem(me + 1, count)
    half = lax.broadcasted_iota(jnp.int32, (1, columns), 1) < rows
    peak = jnp.max(received_ref[:, PACKED - 1, :], axis=0, keepdims=True)
    peak = jnp.where(half, pltpu.roll(peak, rows, 1), peak)
    peak_ref[...] = jnp.broadcast_to(peak[None], peak_ref.shape)

    side_ref[0] = received_ref[after]
    side_ref[1] = pltpu.roll(received_ref[after], rows, 1)
    side_ref[2] = received_ref[before]
    side_ref[3] = pltpu.roll(received_ref[before], rows, 1)
    for k in range(FIELDS):
        at = k * STRIP
        strip_ref[k, :STRIP, :] = own_ref[at : at + STRIP, :]
        strip_ref[k, STRIP:, :] = jnp.broadcast_to(own_ref[at + WIDTH : at + WIDTH + 1, :], (16 - STRIP, columns))
        for j in range(WIDTH):
            slot = k * WIDTH + j
            row, far = slot % PACKED, slot // PACKED
            low, high = at + j, at + 2 * WIDTH + j
            strip_ref[k, j : j + 1, :] = jnp.where(
                half, own_ref[low : low + 1, :], side_ref[2 if far else 3, row : row + 1, :]
            )
            strip_ref[k, 2 * WIDTH + j : 2 * WIDTH + j + 1, :] = jnp.where(
                half, side_ref[1 if far else 0, row : row + 1, :], own_ref[high : high + 1, :]
            )
    edge = flux_difference([strip_ref[k] for k in range(FIELDS)], 0, 1)
    turned_ref[...] = jnp.zeros_like(turned_ref)
    for k in range(FIELDS):
        turned_ref[k * WIDTH : (k + 1) * WIDTH, :] = edge[k][WIDTH : 2 * WIDTH]
    turned = jnp.transpose(turned_ref[...])
    at_end, at_start = turned[:rows], turned[rows:]
    lane = lax.broadcasted_iota(jnp.int32, (rows, columns), 1)
    for k in range(FIELDS):
        change = jnp.where(
            lane >= columns - WIDTH, pltpu.roll(at_end, columns - WIDTH - k * WIDTH, 1), inner_ref[k]
        )
        change = jnp.where(lane < WIDTH, pltpu.roll(at_start, (-k * WIDTH) % columns, 1), change)
        change_ref[k] = change
        at, far = k * WIDTH, (FIELDS + k) * WIDTH
        first_ref[at : at + WIDTH, :] = cells_ref[k, :WIDTH, :]
        last_ref[at : at + WIDTH, :] = cells_ref[k, rows - WIDTH :, :]
        first_ref[far : far + WIDTH, :] = change[:WIDTH]
        last_ref[far : far + WIDTH, :] = change[rows - WIDTH :]
    first_ref[2 * FIELDS * WIDTH :, :] = jnp.zeros((2, columns), jnp.float32)
    last_ref[2 * FIELDS * WIDTH :, :] = jnp.zeros((2, columns), jnp.float32)


def sweep_kernel(cells_ref, change_ref, peaks_ref, before_ref, after_ref, out_ref, half_ref):
    rows, columns = out_ref.shape[1:]
    peak = jnp.max(jnp.max(peaks_ref[...], axis=0), axis=1, keepdims=True)
    time_step = COURANT / peak
    size = FIELDS * WIDTH
    before = before_ref[:size, :] - time_step * before_ref[size : 2 * size, :]
    after = after_ref[:size, :] - time_step * after_ref[size : 2 * size, :]
    for k in range(FIELDS):
        half = cells_ref[k] - time_step * change_ref[k]
        half_ref[k, :rows, :] = half
        half_ref[k, rows : rows + 8, :] = half[:8]
        half_ref[k, rows : rows + WIDTH, :] = after[k * WIDTH : (k + 1) * WIDTH]
        half_ref[k, rows + 8 - WIDTH : rows + 8, :] = before[k * WIDTH : (k + 1) * WIDTH]
    cells = [half_ref[k] for k in range(FIELDS)]
    change = flux_difference(cells, 0, 2)
    for k in range(FIELDS):
        out_ref[k] = (cells[k] - time_step * change[k])[:rows]


def call(kernel, out_shape, n_smem, n_vmem, scratch=()):
    return pl.pallas_call(
        kernel,
        out_shape=out_shape,
        in_specs=[SMEM] * n_smem + [VMEM] * n_vmem,
        out_specs=jax.tree.map(lambda _: VMEM, out_shape),
        scratch_shapes=list(scratch),
        cost_estimate=pl.CostEstimate(flops=4_000_000, bytes_accessed=1_000_000, transcendentals=0),
    )


def f32(*shape):
    return jax.ShapeDtypeStruct(shape, jnp.float32)


def kept(*shape):
    return pltpu.VMEM(shape, jnp.float32)


def held(*arrays):
    return [pltpu.with_memory_space_constraint(array, pltpu.VMEM) for array in arrays]


def local(fields):
    rows, columns = fields.shape[2:]
    fields = fields.reshape(FIELDS, rows, columns)
    count_row, count_col = lax.axis_size(ROW), lax.axis_size(COL)
    me = lax.axis_index(ROW).astype(jnp.int32).reshape(1)
    whole = kept(FIELDS, rows, columns)
    halo = kept(32, columns)
    up = [(i, (i + 1) % count_col) for i in range(count_col)]

    shapes = (kept(count_row, PACKED, columns), kept(48, columns), whole)
    send, own, cells = call(start_kernel, shapes, 1, 1, [pltpu.VMEM((48, columns), jnp.float32)])(me, fields)
    received = lax.all_to_all(send, ROW, 0, 0, tiled=True)
    inner = call(inner_kernel, whole, 0, 1)(*held(cells))
    shapes = (whole, halo, halo, kept(count_col, 1, columns))
    scratch = [(FIELDS, 16, columns), (4, PACKED, columns), (columns, columns)]
    scratch = [pltpu.VMEM(shape, jnp.float32) for shape in scratch]
    change, first, last, peak = call(edge_kernel, shapes, 1, 4, scratch)(
        me, *held(cells, inner, own, received)
    )
    peaks = lax.all_to_all(peak, COL, 0, 0, tiled=True)
    before = lax.ppermute(last, COL, up)
    after = lax.ppermute(first, COL, [(j, i) for i, j in up])
    scratch = [pltpu.VMEM((FIELDS, rows + 8, columns), jnp.float32)]
    out = call(sweep_kernel, f32(FIELDS, rows, columns), 0, 5, scratch)(
        *held(cells, change, peaks, before, after)
    )
    return out.reshape(FIELDS, 1, rows, columns)


def solution(mesh):
    split = Mesh(mesh.devices.reshape(8, 2, 8, 4, 2), (*ROW, *COL))
    placed = (P(None, None, COL, ROW),)
    return jax.shard_map(
        local, mesh=split, in_specs=placed, out_specs=P(None, None, COL, ROW), check_vma=False
    )
```

time: 57.1 us -> 57.1 us (level)
  the two profiles are of different devices: /device:TPU:8 before, /device:TPU:1 now
where the time goes in v3:
time: 57.1 us; the launch traced here: 56.8 us
  starting transfers between devices  39.7 us (70%)
  waiting for transfers between devices  12.7 us (22%)
  Pallas kernels  4.27 us (7%)
    all_to_all x1, starting transfers between devices, local(): peaks = lax.all_to_all(peak, COL, 0, 0, tiled=True)  22.4 us
    all_to_all x1, starting transfers between devices, local(): received = lax.all_to_all(send, ROW, 0, 0, tiled=True)  10.9 us
    all_to_all x1, waiting for transfers between devices, local(): received = lax.all_to_all(send, ROW, 0, 0, tiled=True)  7.4 us
    ppermute x1, starting transfers between devices, local(): before = lax.ppermute(last, COL, up)  4.44 us
    ppermute x1, waiting for transfers between devices, local(): after = lax.ppermute(first, COL, [(j, i) for i, j in up])  4.32 us
    ppermute x1, starting transfers between devices, local(): after = lax.ppermute(first, COL, [(j, i) for i, j in up])  1.92 us
    pallas_call x1, Pallas kernels, local(): call(start_kernel, shapes, 1, 1, [pltpu.VMEM((48, columns), jnp.float32)])  1.84 us
    pallas_call x1, Pallas kernels, local(): call(sweep_kernel, f32(FIELDS, rows, columns), 0, 5, scratch)  1.18 us
  transfers between devices with their start and end apart: 4, of which 3 were waited for; matrix products, arithmetic and copies ran while one was open for 0% of the time, Pallas kernels for 1%

profile of v3, /device:TPU:1, one launch (start us, length us, event | category | flops | bytes accessed | tf_op | source)
XLA Modules:
  0.0 56.8 jit_solution(1895217460103770685)
XLA Ops:
  0.0 1.8 %shard_map.17 = (f32[16,8,128]{2,1,0:T(8,128)}, f32[48,128]{1,0:T(8,128)S(1)}, f32[5,64,128]{2,1,0:T(8,128)S(1)}) custom-call(s32[1]{0:T(128)} %bitcast.me_ref, f32[5,64,128]{2,1,0:T(8,128)} %bitcast.5), custom_call_target="tpu_custom_call" | custom-call | flops 4000000 | bytes 1000000 | tf_op jit(solution)/shard_map/pallas_call | solution.py:235
  1.8 10.9 %all-to-all-start = ((f32[16,8,128]{2,1,0:T(8,128)}), f32[16,8,128]{2,1,0:T(8,128)S(1)}, u32[]{:S(2)}, u32[]{:S(2)}) async-start(f32[16,8,128]{2,1,0:T(8,128)} %get-tuple-element.14), calls=%async_computation | async-start | bytes 131072 | tf_op jit(solution)/shard_map/all_to_all | solution.py:236
  12.8 0.5 shard_map.18.inner_ref
  13.3 7.4 %all-to-all-done.received_ref = f32[16,8,128]{2,1,0:T(8,128)S(1)} async-done(((f32[16,8,128]{2,1,0:T(8,128)}), f32[16,8,128]{2,1,0:T(8,128)S(1)}, u32[]{:S(2)}, u32[]{:S(2)}) %all-to-all-start) | async-done | bytes 65568 | tf_op jit(solution)/shard_map/all_to_all | solution.py:236
  20.7 0.8 %shard_map.19 = (f32[5,64,128]{2,1,0:T(8,128)S(1)}, f32[32,128]{1,0:T(8,128)S(1)}, f32[32,128]{1,0:T(8,128)S(1)}, f32[64,1,128]{2,1,0:T(1,128)}) custom-call(s32[1]{0:T(128)} %bitcast.me_ref, f32[5,64,128]{2,1,0:T(8,128)S(1)} %get-tuple-element.12.cells_ref, f32[5,64,128]{2,1,0:T(8,128)S(1)} %shard_map.18.inner_ref, ...), custom_call_target="tpu_custom_call" | custom-call | flops 4000000 | bytes 1000000 | tf_op jit(solution)/shard_map/pallas_call | solution.py:241
  21.4 22.4 %all-to-all-start.1 = ((f32[64,1,128]{2,1,0:T(1,128)}), f32[64,1,128]{2,1,0:T(1,128)S(1)}, u32[]{:S(2)}, u32[]{:S(2)}) async-start(f32[64,1,128]{2,1,0:T(1,128)} %get-tuple-element.16), calls=%async_computation.1 | async-start | bytes 65536 | tf_op jit(solution)/shard_map/all_to_all | solution.py:244
  43.9 4.4 %collective-permute-start = (f32[32,128]{1,0:T(8,128)S(1)}, f32[32,128]{1,0:T(8,128)S(1)}, u32[]{:S(2)}, u32[]{:S(2)}) collective-permute-start(f32[32,128]{1,0:T(8,128)S(1)} %get-tuple-element.17), channel_id=1, source_target_pairs={{0,1},{1,2},{2,3},{3,4},{4,5},{5,6},{6,7},{7,8},{8,9},{9,10},{10,1... | collective-permute-start | bytes 49160 | tf_op jit(solution)/shard_map/ppermute | solution.py:245
  48.3 1.9 %collective-permute-start.1 = (f32[32,128]{1,0:T(8,128)S(1)}, f32[32,128]{1,0:T(8,128)S(1)}, u32[]{:S(2)}, u32[]{:S(2)}) collective-permute-start(f32[32,128]{1,0:T(8,128)S(1)} %get-tuple-element.18), channel_id=1, source_target_pairs={{1,0},{2,1},{3,2},{4,3},{5,4},{6,5},{7,6},{8,7},{9,8},{10,9},{11,1... | collective-permute-start | bytes 49160 | tf_op jit(solution)/shard_map/ppermute | solution.py:246
  50.3 0.0 collective-permute-done.before_ref
  50.3 4.3 %collective-permute-done.1.after_ref = f32[32,128]{1,0:T(8,128)S(1)} collective-permute-done((f32[32,128]{1,0:T(8,128)S(1)}, f32[32,128]{1,0:T(8,128)S(1)}, u32[]{:S(2)}, u32[]{:S(2)}) %collective-permute-start.1) | collective-permute-done | bytes 16416 | tf_op jit(solution)/shard_map/ppermute | solution.py:246
  54.6 1.0 %all-to-all-done.1.peaks_ref = f32[64,1,128]{2,1,0:T(1,128)S(1)} async-done(((f32[64,1,128]{2,1,0:T(1,128)}), f32[64,1,128]{2,1,0:T(1,128)S(1)}, u32[]{:S(2)}, u32[]{:S(2)}) %all-to-all-start.1) | async-done | bytes 32800 | tf_op jit(solution)/shard_map/all_to_all | solution.py:244
  55.6 1.2 %shard_map.20 = f32[5,64,128]{2,1,0:T(8,128)} custom-call(f32[5,64,128]{2,1,0:T(8,128)S(1)} %get-tuple-element.12.cells_ref, f32[5,64,128]{2,1,0:T(8,128)S(1)} %get-tuple-element.15.change_ref, f32[64,1,128]{2,1,0:T(1,128)S(1)} %all-to-all-done.1.peaks_ref, f32[32,128]{1,0:T(8,128)S(1)} %collective-permute-done.before_ref, ...), custom_call_target="tpu_custom_call" | custom-call | flops 4000000 | bytes 1000000 | tf_op jit(solution)/shard_map/pallas_call | solution.py:248
Async XLA Ops:
  1.8 18.8 %all-to-all-start = ((f32[16,8,128]{2,1,0:T(8,128)}), f32[16,8,128]{2,1,0:T(8,128)S(1)}, u32[]{:S(2)}, u32[]{:S(2)}) async-start(f32[16,8,128]{2,1,0:T(8,128)} %get-tuple-element.14), calls=%async_computation | async-start | bytes 131072 | tf_op jit(solution)/shard_map/all_to_all | solution.py:236
  21.4 34.2 %all-to-all-start.1 = ((f32[64,1,128]{2,1,0:T(1,128)}), f32[64,1,128]{2,1,0:T(1,128)S(1)}, u32[]{:S(2)}, u32[]{:S(2)}) async-start(f32[64,1,128]{2,1,0:T(1,128)} %get-tuple-element.16), calls=%async_computation.1 | async-start | bytes 65536 | tf_op jit(solution)/shard_map/all_to_all | solution.py:244
  43.9 6.4 %collective-permute-start = (f32[32,128]{1,0:T(8,128)S(1)}, f32[32,128]{1,0:T(8,128)S(1)}, u32[]{:S(2)}, u32[]{:S(2)}) collective-permute-start(f32[32,128]{1,0:T(8,128)S(1)} %get-tuple-element.17), channel_id=1, source_target_pairs={{0,1},{1,2},{2,3},{3,4},{4,5},{5,6},{6,7},{7,8},{8,9},{9,10},{10,1... | collective-permute-start | bytes 49160 | tf_op jit(solution)/shard_map/ppermute | solution.py:245
  48.3 6.3 %collective-permute-start.1 = (f32[32,128]{1,0:T(8,128)S(1)}, f32[32,128]{1,0:T(8,128)S(1)}, u32[]{:S(2)}, u32[]{:S(2)}) collective-permute-start(f32[32,128]{1,0:T(8,128)S(1)} %get-tuple-element.18), channel_id=1, source_target_pairs={{1,0},{2,1},{3,2},{4,3},{5,4},{6,5},{7,6},{8,7},{9,8},{10,9},{11,1... | collective-permute-start | bytes 49160 | tf_op jit(solution)/shard_map/ppermute | solution.py:246

commit v4 on v3

--- a/solution.py
+++ b/solution.py
@@ -117,7 +117,7 @@
     ends, starts = jnp.concatenate(ends, axis=0), jnp.concatenate(starts, axis=0)
     for j in range(count):
         send_ref[j] = ends
-    send_ref[lax.rem(me_ref[0] + count - 1, count)] = starts
+    send_ref[lax.rem(me_ref[0] // 2 + count - 1, count)] = starts
 
 
 def inner_kernel(cells_ref, change_ref):
@@ -129,11 +129,11 @@
 
 def edge_kernel(
     me_ref, cells_ref, inner_ref, own_ref, received_ref,
-    change_ref, first_ref, last_ref, peak_ref, strip_ref, side_ref, turned_ref,
+    change_ref, near_ref, far_ref, peak_ref, strip_ref, side_ref, turned_ref,
 ):
     count = received_ref.shape[0]
     rows, columns = cells_ref.shape[1:]
-    me = me_ref[0]
+    me, odd = me_ref[0] // 2, lax.rem(me_ref[0], 2) == 1
     before, after = lax.rem(me + count - 1, count), lax.rem(me + 1, count)
     half = lax.broadcasted_iota(jnp.int32, (1, columns), 1) < rows
     peak = jnp.max(received_ref[:, PACKED - 1, :], axis=0, keepdims=True)
@@ -171,22 +171,24 @@
         )
         change = jnp.where(lane < WIDTH, pltpu.roll(at_start, (-k * WIDTH) % columns, 1), change)
         change_ref[k] = change
-        at, far = k * WIDTH, (FIELDS + k) * WIDTH
-        first_ref[at : at + WIDTH, :] = cells_ref[k, :WIDTH, :]
-        last_ref[at : at + WIDTH, :] = cells_ref[k, rows - WIDTH :, :]
-        first_ref[far : far + WIDTH, :] = change[:WIDTH]
-        last_ref[far : far + WIDTH, :] = change[rows - WIDTH :]
-    first_ref[2 * FIELDS * WIDTH :, :] = jnp.zeros((2, columns), jnp.float32)
-    last_ref[2 * FIELDS * WIDTH :, :] = jnp.zeros((2, columns), jnp.float32)
-
-
-def sweep_kernel(cells_ref, change_ref, peaks_ref, before_ref, after_ref, out_ref, half_ref):
+        ends = [(cells_ref[k, :WIDTH, :], cells_ref[k, rows - WIDTH :, :]), (change[:WIDTH], change[rows - WIDTH :])]
+        for part, (first, last) in enumerate(ends):
+            at = (part * FIELDS + k) * WIDTH
+            near_ref[at : at + WIDTH, :] = jnp.where(odd, first, last)
+            far_ref[at : at + WIDTH, :] = jnp.where(odd, last, first)
+    near_ref[2 * FIELDS * WIDTH :, :] = jnp.zeros((2, columns), jnp.float32)
+    far_ref[2 * FIELDS * WIDTH :, :] = jnp.zeros((2, columns), jnp.float32)
+
+
+def sweep_kernel(me_ref, cells_ref, change_ref, peaks_ref, near_ref, far_ref, out_ref, half_ref):
     rows, columns = out_ref.shape[1:]
     peak = jnp.max(jnp.max(peaks_ref[...], axis=0), axis=1, keepdims=True)
     time_step = COURANT / peak
     size = FIELDS * WIDTH
-    before = before_ref[:size, :] - time_step * before_ref[size : 2 * size, :]
-    after = after_ref[:size, :] - time_step * after_ref[size : 2 * size, :]
+    odd = lax.rem(me_ref[0], 2) == 1
+    near = near_ref[:size, :] - time_step * near_ref[size : 2 * size, :]
+    far = far_ref[:size, :] - time_step * far_ref[size : 2 * size, :]
+    before, after = jnp.where(odd, near, far), jnp.where(odd, far, near)
     for k in range(FIELDS):
         half = cells_ref[k] - time_step * change_ref[k]
         half_ref[k, :rows, :] = half
@@ -226,10 +228,11 @@
     rows, columns = fields.shape[2:]
     fields = fields.reshape(FIELDS, rows, columns)
     count_row, count_col = lax.axis_size(ROW), lax.axis_size(COL)
-    me = lax.axis_index(ROW).astype(jnp.int32).reshape(1)
+    me = (lax.axis_index(ROW) * 2 + lax.axis_index(COL[-1])).astype(jnp.int32).reshape(1)
     whole = kept(FIELDS, rows, columns)
     halo = kept(32, columns)
-    up = [(i, (i + 1) % count_col) for i in range(count_col)]
+    inside = [(i, i ^ 1) for i in range(count_col)]
+    between = [(i, (i + (1 if i % 2 else -1)) % count_col) for i in range(count_col)]
 
     shapes = (kept(count_row, PACKED, columns), kept(48, columns), whole)
     send, own, cells = call(start_kernel, shapes, 1, 1, [pltpu.VMEM((48, columns), jnp.float32)])(me, fields)
@@ -238,15 +241,15 @@
     shapes = (whole, halo, halo, kept(count_col, 1, columns))
     scratch = [(FIELDS, 16, columns), (4, PACKED, columns), (columns, columns)]
     scratch = [pltpu.VMEM(shape, jnp.float32) for shape in scratch]
-    change, first, last, peak = call(edge_kernel, shapes, 1, 4, scratch)(
+    change, near, far, peak = call(edge_kernel, shapes, 1, 4, scratch)(
         me, *held(cells, inner, own, received)
     )
     peaks = lax.all_to_all(peak, COL, 0, 0, tiled=True)
-    before = lax.ppermute(last, COL, up)
-    after = lax.ppermute(first, COL, [(j, i) for i, j in up])
+    far = lax.ppermute(far, COL, between)
+    near = lax.ppermute(near, COL, inside)
     scratch = [pltpu.VMEM((FIELDS, rows + 8, columns), jnp.float32)]
-    out = call(sweep_kernel, f32(FIELDS, rows, columns), 0, 5, scratch)(
-        *held(cells, change, peaks, before, after)
+    out = call(sweep_kernel, f32(FIELDS, rows, columns), 1, 5, scratch)(
+        me, *held(cells, change, peaks, near, far)
     )
     return out.reshape(FIELDS, 1, rows, columns)
 

time: 57.1 us -> 57.3 us (level)
    ppermute x2, waiting for transfers between devices: 4.33 us -> 2.34 us  [the longest x1 2.34 us: local(): far = lax.ppermute(far, COL, between)]
    all_to_all x1, waiting for transfers between devices: 1.02 us -> 2.9 us  [local(): peaks = lax.all_to_all(peak, COL, 0, 0, tiled=True)]
where the time goes in v4:
time: 57.3 us; the launch traced here: 57 us
  starting transfers between devices  39.8 us (69%)
  waiting for transfers between devices  12.6 us (22%)
  Pallas kernels  4.48 us (8%)
    all_to_all x1, starting transfers between devices, local(): peaks = lax.all_to_all(peak, COL, 0, 0, tiled=True)  22.4 us
    all_to_all x1, starting transfers between devices, local(): received = lax.all_to_all(send, ROW, 0, 0, tiled=True)  10.9 us
    all_to_all x1, waiting for transfers between devices, local(): received = lax.all_to_all(send, ROW, 0, 0, tiled=True)  7.4 us
    ppermute x1, starting transfers between devices, local(): far = lax.ppermute(far, COL, between)  4.1 us
    all_to_all x1, waiting for transfers between devices, local(): peaks = lax.all_to_all(peak, COL, 0, 0, tiled=True)  2.9 us
    ppermute x1, starting transfers between devices, local(): near = lax.ppermute(near, COL, inside)  2.36 us
    ppermute x1, waiting for transfers between devices, local(): far = lax.ppermute(far, COL, between)  2.34 us
    pallas_call x1, Pallas kernels, local(): call(start_kernel, shapes, 1, 1, [pltpu.VMEM((48, columns), jnp.float32)])  1.84 us
  transfers between devices with their start and end apart: 4, of which 3 were waited for; matrix products, arithmetic and copies ran while one was open for 0% of the time, Pallas kernels for 1%

profile of v4, /device:TPU:1, one launch (start us, length us, event | category | flops | bytes accessed | tf_op | source)
XLA Modules:
  0.0 57.0 jit_solution(17254053512912439293)
XLA Ops:
  0.0 1.8 %shard_map.17 = (f32[16,8,128]{2,1,0:T(8,128)}, f32[48,128]{1,0:T(8,128)S(1)}, f32[5,64,128]{2,1,0:T(8,128)S(1)}) custom-call(s32[1]{0:T(128)} %bitcast.me_ref, f32[5,64,128]{2,1,0:T(8,128)} %bitcast.5), custom_call_target="tpu_custom_call" | custom-call | flops 4000000 | bytes 1000000 | tf_op jit(solution)/shard_map/pallas_call | solution.py:238
  1.8 10.9 %all-to-all-start = ((f32[16,8,128]{2,1,0:T(8,128)}), f32[16,8,128]{2,1,0:T(8,128)S(1)}, u32[]{:S(2)}, u32[]{:S(2)}) async-start(f32[16,8,128]{2,1,0:T(8,128)} %get-tuple-element.14), calls=%async_computation | async-start | bytes 131072 | tf_op jit(solution)/shard_map/all_to_all | solution.py:239
  12.8 0.5 shard_map.18.inner_ref
  13.3 7.4 %all-to-all-done.received_ref = f32[16,8,128]{2,1,0:T(8,128)S(1)} async-done(((f32[16,8,128]{2,1,0:T(8,128)}), f32[16,8,128]{2,1,0:T(8,128)S(1)}, u32[]{:S(2)}, u32[]{:S(2)}) %all-to-all-start) | async-done | bytes 65568 | tf_op jit(solution)/shard_map/all_to_all | solution.py:239
  20.7 1.0 %shard_map.19 = (f32[5,64,128]{2,1,0:T(8,128)S(1)}, f32[32,128]{1,0:T(8,128)S(1)}, f32[32,128]{1,0:T(8,128)S(1)}, f32[64,1,128]{2,1,0:T(1,128)}) custom-call(s32[1]{0:T(128)} %bitcast.me_ref, f32[5,64,128]{2,1,0:T(8,128)S(1)} %get-tuple-element.12.cells_ref, f32[5,64,128]{2,1,0:T(8,128)S(1)} %shard_map.18.inner_ref, ...), custom_call_target="tpu_custom_call" | custom-call | flops 4000000 | bytes 1000000 | tf_op jit(solution)/shard_map/pallas_call | solution.py:244
  21.6 22.4 %all-to-all-start.1 = ((f32[64,1,128]{2,1,0:T(1,128)}), f32[64,1,128]{2,1,0:T(1,128)S(1)}, u32[]{:S(2)}, u32[]{:S(2)}) async-start(f32[64,1,128]{2,1,0:T(1,128)} %get-tuple-element.16), calls=%async_computation.1 | async-start | bytes 65536 | tf_op jit(solution)/shard_map/all_to_all | solution.py:247
  44.1 2.4 %collective-permute-start = (f32[32,128]{1,0:T(8,128)S(1)}, f32[32,128]{1,0:T(8,128)S(1)}, u32[]{:S(2)}, u32[]{:S(2)}) collective-permute-start(f32[32,128]{1,0:T(8,128)S(1)} %get-tuple-element.17), channel_id=1, source_target_pairs={{0,1},{1,0},{2,3},{3,2},{4,5},{5,4},{6,7},{7,6},{8,9},{9,8},{10,11... | collective-permute-start | bytes 49160 | tf_op jit(solution)/shard_map/ppermute | solution.py:249
  46.5 4.1 %collective-permute-start.1 = (f32[32,128]{1,0:T(8,128)S(1)}, f32[32,128]{1,0:T(8,128)S(1)}, u32[]{:S(2)}, u32[]{:S(2)}) collective-permute-start(f32[32,128]{1,0:T(8,128)S(1)} %get-tuple-element.18), channel_id=1, source_target_pairs={{0,63},{1,2},{2,1},{3,4},{4,3},{5,6},{6,5},{7,8},{8,7},{9,10},{10,... | collective-permute-start | bytes 49160 | tf_op jit(solution)/shard_map/ppermute | solution.py:248
  50.6 0.0 collective-permute-done.near_ref
  50.6 2.3 %collective-permute-done.1.far_ref = f32[32,128]{1,0:T(8,128)S(1)} collective-permute-done((f32[32,128]{1,0:T(8,128)S(1)}, f32[32,128]{1,0:T(8,128)S(1)}, u32[]{:S(2)}, u32[]{:S(2)}) %collective-permute-start.1) | collective-permute-done | bytes 16416 | tf_op jit(solution)/shard_map/ppermute | solution.py:248
  52.9 2.9 %all-to-all-done.1.peaks_ref = f32[64,1,128]{2,1,0:T(1,128)S(1)} async-done(((f32[64,1,128]{2,1,0:T(1,128)}), f32[64,1,128]{2,1,0:T(1,128)S(1)}, u32[]{:S(2)}, u32[]{:S(2)}) %all-to-all-start.1) | async-done | bytes 32800 | tf_op jit(solution)/shard_map/all_to_all | solution.py:247
  55.8 1.2 %shard_map.20 = f32[5,64,128]{2,1,0:T(8,128)} custom-call(s32[1]{0:T(128)} %bitcast.me_ref, f32[5,64,128]{2,1,0:T(8,128)S(1)} %get-tuple-element.12.cells_ref, f32[5,64,128]{2,1,0:T(8,128)S(1)} %get-tuple-element.15.change_ref, f32[64,1,128]{2,1,0:T(1,128)S(1)} %all-to-all-done.1.peaks_ref, f32[32,128]{1,0:T(8,128)S(1)} %collective-permute-done.near_ref, ...), custom_call_target="tpu_custom_call" | custom-call | flops 4000000 | bytes 1000000 | tf_op jit(solution)/shard_map/pallas_call | solution.py:251
Async XLA Ops:
  1.8 18.8 %all-to-all-start = ((f32[16,8,128]{2,1,0:T(8,128)}), f32[16,8,128]{2,1,0:T(8,128)S(1)}, u32[]{:S(2)}, u32[]{:S(2)}) async-start(f32[16,8,128]{2,1,0:T(8,128)} %get-tuple-element.14), calls=%async_computation | async-start | bytes 131072 | tf_op jit(solution)/shard_map/all_to_all | solution.py:239
  21.6 34.2 %all-to-all-start.1 = ((f32[64,1,128]{2,1,0:T(1,128)}), f32[64,1,128]{2,1,0:T(1,128)S(1)}, u32[]{:S(2)}, u32[]{:S(2)}) async-start(f32[64,1,128]{2,1,0:T(1,128)} %get-tuple-element.16), calls=%async_computation.1 | async-start | bytes 65536 | tf_op jit(solution)/shard_map/all_to_all | solution.py:247
  44.1 6.5 %collective-permute-start = (f32[32,128]{1,0:T(8,128)S(1)}, f32[32,128]{1,0:T(8,128)S(1)}, u32[]{:S(2)}, u32[]{:S(2)}) collective-permute-start(f32[32,128]{1,0:T(8,128)S(1)} %get-tuple-element.17), channel_id=1, source_target_pairs={{0,1},{1,0},{2,3},{3,2},{4,5},{5,4},{6,7},{7,6},{8,9},{9,8},{10,11... | collective-permute-start | bytes 49160 | tf_op jit(solution)/shard_map/ppermute | solution.py:249
  46.5 6.5 %collective-permute-start.1 = (f32[32,128]{1,0:T(8,128)S(1)}, f32[32,128]{1,0:T(8,128)S(1)}, u32[]{:S(2)}, u32[]{:S(2)}) collective-permute-start(f32[32,128]{1,0:T(8,128)S(1)} %get-tuple-element.18), channel_id=1, source_target_pairs={{0,63},{1,2},{2,1},{3,4},{4,3},{5,6},{6,5},{7,8},{8,7},{9,10},{10,... | collective-permute-start | bytes 49160 | tf_op jit(solution)/shard_map/ppermute | solution.py:248

commit v5 on v4

--- a/solution.py
+++ b/solution.py
@@ -5,6 +5,7 @@
 from jax.experimental.pallas import tpu as pltpu
 from jax.sharding import Mesh
 from jax.sharding import PartitionSpec as P
+
 
 ROW = ("row_0", "row_1")
 COL = ("col_0", "col_1", "col_2")
@@ -127,19 +128,24 @@
             change_ref[k, row : row + 8, :] = change[k]
 
 
+def peak_kernel(received_ref, peak_ref):
+    columns = received_ref.shape[2]
+    rows = columns // 2
+    half = lax.broadcasted_iota(jnp.int32, (1, columns), 1) < rows
+    peak = jnp.max(received_ref[...], axis=0)[PACKED - 1 :, :]
+    peak = jnp.where(half, pltpu.roll(peak, rows, 1), peak)
+    peak_ref[...] = jnp.broadcast_to(peak[None], peak_ref.shape)
+
+
 def edge_kernel(
     me_ref, cells_ref, inner_ref, own_ref, received_ref,
-    change_ref, near_ref, far_ref, peak_ref, strip_ref, side_ref, turned_ref,
+    change_ref, near_ref, far_ref, strip_ref, side_ref, turned_ref,
 ):
     count = received_ref.shape[0]
     rows, columns = cells_ref.shape[1:]
     me, odd = me_ref[0] // 2, lax.rem(me_ref[0], 2) == 1
     before, after = lax.rem(me + count - 1, count), lax.rem(me + 1, count)
     half = lax.broadcasted_iota(jnp.int32, (1, columns), 1) < rows
-    peak = jnp.max(received_ref[:, PACKED - 1, :], axis=0, keepdims=True)
-    peak = jnp.where(half, pltpu.roll(peak, rows, 1), peak)
-    peak_ref[...] = jnp.broadcast_to(peak[None], peak_ref.shape)
-
     side_ref[0] = received_ref[after]
     side_ref[1] = pltpu.roll(received_ref[after], rows, 1)
     side_ref[2] = received_ref[before]
@@ -181,7 +187,7 @@
 
 
 def sweep_kernel(me_ref, cells_ref, change_ref, peaks_ref, near_ref, far_ref, out_ref, half_ref):
-    rows, columns = out_ref.shape[1:]
+    rows, _ = out_ref.shape[1:]
     peak = jnp.max(jnp.max(peaks_ref[...], axis=0), axis=1, keepdims=True)
     time_step = COURANT / peak
     size = FIELDS * WIDTH
@@ -235,16 +241,15 @@
     between = [(i, (i + (1 if i % 2 else -1)) % count_col) for i in range(count_col)]
 
     shapes = (kept(count_row, PACKED, columns), kept(48, columns), whole)
-    send, own, cells = call(start_kernel, shapes, 1, 1, [pltpu.VMEM((48, columns), jnp.float32)])(me, fields)
+    scratch = [pltpu.VMEM((48, columns), jnp.float32)]
+    send, own, cells = call(start_kernel, shapes, 1, 1, scratch)(me, fields)
     received = lax.all_to_all(send, ROW, 0, 0, tiled=True)
     inner = call(inner_kernel, whole, 0, 1)(*held(cells))
-    shapes = (whole, halo, halo, kept(count_col, 1, columns))
+    peak = call(peak_kernel, kept(count_col, 1, columns), 0, 1)(*held(received))
+    peaks = lax.all_to_all(peak, COL, 0, 0, tiled=True)
     scratch = [(FIELDS, 16, columns), (4, PACKED, columns), (columns, columns)]
     scratch = [pltpu.VMEM(shape, jnp.float32) for shape in scratch]
-    change, near, far, peak = call(edge_kernel, shapes, 1, 4, scratch)(
-        me, *held(cells, inner, own, received)
-    )
-    peaks = lax.all_to_all(peak, COL, 0, 0, tiled=True)
+    change, near, far = call(edge_kernel, (whole, halo, halo), 1, 4, scratch)(me, *held(cells, inner, own, received))
     far = lax.ppermute(far, COL, between)
     near = lax.ppermute(near, COL, inside)
     scratch = [pltpu.VMEM((FIELDS, rows + 8, columns), jnp.float32)]

time: 57.3 us -> 56.2 us (0.981)
  blocking collectives: 0 us -> 18.6 us
  starting transfers between devices: 39.8 us -> 28.9 us
  waiting for transfers between devices: 12.6 us -> 4.34 us
    all_to_all x0 -> x1, blocking collectives: none -> 18.6 us  [local(): received = lax.all_to_all(send, ROW, 0, 0, tiled=True)]
    all_to_all x1 -> x0, starting transfers between devices: 10.9 us -> none  [local(): received = lax.all_to_all(send, ROW, 0, 0, tiled=True)]
    all_to_all x1 -> x0, waiting for transfers between devices: 7.4 us -> none  [local(): received = lax.all_to_all(send, ROW, 0, 0, tiled=True)]
    all_to_all x1, waiting for transfers between devices: 2.9 us -> 2.19 us  [local(): peaks = lax.all_to_all(peak, COL, 0, 0, tiled=True)]
    pallas_call x2 -> x3, Pallas kernels: 2.81 us -> 2.32 us  [the longest x1 1.2 us: local(): send, own, cells = call(start_kernel, shapes, 1, 1, scratch)(me, fields)]
  transfers between devices with their start and end apart: 4 -> 3, of which waited for: 3 -> 2; matrix products, arithmetic and copies ran while one was open for 0% -> 0% of each run, Pallas kernels for 1% -> 2%
where the time goes in v5:
time: 56.2 us; the launch traced here: 55.9 us
  starting transfers between devices  28.9 us (51%)
  blocking collectives  18.6 us (33%)
  waiting for transfers between devices  4.34 us (8%)
  Pallas kernels  3.99 us (7%)
    all_to_all x1, starting transfers between devices, local(): peaks = lax.all_to_all(peak, COL, 0, 0, tiled=True)  22.4 us
    all_to_all x1, blocking collectives, local(): received = lax.all_to_all(send, ROW, 0, 0, tiled=True)  18.6 us
    ppermute x1, starting transfers between devices, local(): far = lax.ppermute(far, COL, between)  4.1 us
    ppermute x1, starting transfers between devices, local(): near = lax.ppermute(near, COL, inside)  2.36 us
    all_to_all x1, waiting for transfers between devices, local(): peaks = lax.all_to_all(peak, COL, 0, 0, tiled=True)  2.19 us
    ppermute x1, waiting for transfers between devices, local(): far = lax.ppermute(far, COL, between)  2.14 us
    pallas_call x1, Pallas kernels, local(): send, own, cells = call(start_kernel, shapes, 1, 1, scratch)(me, fields)  1.2 us
    pallas_call x1, Pallas kernels, local(): call(sweep_kernel, f32(FIELDS, rows, columns), 1, 5, scratch)  1.18 us
  transfers between devices with their start and end apart: 3, of which 2 were waited for; matrix products, arithmetic and copies ran while one was open for 0% of the time, Pallas kernels for 2%

profile of v5, /device:TPU:1, one launch (start us, length us, event | category | flops | bytes accessed | tf_op | source)
XLA Modules:
  0.0 55.9 jit_solution(1230433264815812617)
XLA Ops:
  0.0 1.2 %shard_map.17 = (f32[16,8,128]{2,1,0:T(8,128)S(1)}, f32[48,128]{1,0:T(8,128)S(1)}, f32[5,64,128]{2,1,0:T(8,128)S(1)}) custom-call(s32[1]{0:T(128)} %bitcast.me_ref, f32[5,64,128]{2,1,0:T(8,128)} %bitcast.5), custom_call_target="tpu_custom_call" | custom-call | flops 4000000 | bytes 1000000 | tf_op jit(solution)/shard_map/pallas_call | solution.py:245
  1.2 18.6 %all_to_all.10.received_ref = f32[16,8,128]{2,1,0:T(8,128)S(1)} all-to-all(f32[16,8,128]{2,1,0:T(8,128)S(1)} %get-tuple-element.13), channel_id=1, replica_groups=mesh['row_0'=8,'row_1'=2,'col_0'=8,'col_1'=4,'col_2'=2] {'row_0','row_1'}, dimensions={0} | all-to-all | bytes 131072 | tf_op jit(solution)/shard_map/all_to_all | solution.py:246
  19.8 0.7 %shard_map.20 = f32[64,1,128]{2,1,0:T(1,128)} custom-call(f32[16,8,128]{2,1,0:T(8,128)S(1)} %all_to_all.10.received_ref), custom_call_target="tpu_custom_call" | custom-call | flops 4000000 | bytes 1000000 | tf_op jit(solution)/shard_map/pallas_call | solution.py:248
  20.5 22.4 %all-to-all-start.1 = ((f32[64,1,128]{2,1,0:T(1,128)}), f32[64,1,128]{2,1,0:T(1,128)S(1)}, u32[]{:S(2)}, u32[]{:S(2)}) async-start(f32[64,1,128]{2,1,0:T(1,128)} %shard_map.20), calls=%async_computation.1 | async-start | bytes 65536 | tf_op jit(solution)/shard_map/all_to_all | solution.py:249
  43.0 0.5 shard_map.18.inner_ref
  43.5 0.4 shard_map.19
  43.9 2.4 %collective-permute-start = (f32[32,128]{1,0:T(8,128)S(1)}, f32[32,128]{1,0:T(8,128)S(1)}, u32[]{:S(2)}, u32[]{:S(2)}) collective-permute-start(f32[32,128]{1,0:T(8,128)S(1)} %get-tuple-element.15), channel_id=1, source_target_pairs={{0,1},{1,0},{2,3},{3,2},{4,5},{5,4},{6,7},{7,6},{8,9},{9,8},{10,11... | collective-permute-start | bytes 49160 | tf_op jit(solution)/shard_map/ppermute | solution.py:254
  46.3 4.1 %collective-permute-start.1 = (f32[32,128]{1,0:T(8,128)S(1)}, f32[32,128]{1,0:T(8,128)S(1)}, u32[]{:S(2)}, u32[]{:S(2)}) collective-permute-start(f32[32,128]{1,0:T(8,128)S(1)} %get-tuple-element.16), channel_id=1, source_target_pairs={{0,63},{1,2},{2,1},{3,4},{4,3},{5,6},{6,5},{7,8},{8,7},{9,10},{10,... | collective-permute-start | bytes 49160 | tf_op jit(solution)/shard_map/ppermute | solution.py:253
  50.4 0.0 collective-permute-done.near_ref
  50.4 2.1 %collective-permute-done.1.far_ref = f32[32,128]{1,0:T(8,128)S(1)} collective-permute-done((f32[32,128]{1,0:T(8,128)S(1)}, f32[32,128]{1,0:T(8,128)S(1)}, u32[]{:S(2)}, u32[]{:S(2)}) %collective-permute-start.1) | collective-permute-done | bytes 16416 | tf_op jit(solution)/shard_map/ppermute | solution.py:253
  52.5 2.2 %all-to-all-done.1.peaks_ref = f32[64,1,128]{2,1,0:T(1,128)S(1)} async-done(((f32[64,1,128]{2,1,0:T(1,128)}), f32[64,1,128]{2,1,0:T(1,128)S(1)}, u32[]{:S(2)}, u32[]{:S(2)}) %all-to-all-start.1) | async-done | bytes 32800 | tf_op jit(solution)/shard_map/all_to_all | solution.py:249
  54.7 1.2 %shard_map.21 = f32[5,64,128]{2,1,0:T(8,128)} custom-call(s32[1]{0:T(128)} %bitcast.me_ref, f32[5,64,128]{2,1,0:T(8,128)S(1)} %get-tuple-element.11.cells_ref, f32[5,64,128]{2,1,0:T(8,128)S(1)} %get-tuple-element.14.change_ref, f32[64,1,128]{2,1,0:T(1,128)S(1)} %all-to-all-done.1.peaks_ref, f32[32,128]{1,0:T(8,128)S(1)} %collective-permute-done.near_ref, ...), custom_call_target="tpu_custom_call" | custom-call | flops 4000000 | bytes 1000000 | tf_op jit(solution)/shard_map/pallas_call | solution.py:256
Async XLA Ops:
  20.5 34.2 %all-to-all-start.1 = ((f32[64,1,128]{2,1,0:T(1,128)}), f32[64,1,128]{2,1,0:T(1,128)S(1)}, u32[]{:S(2)}, u32[]{:S(2)}) async-start(f32[64,1,128]{2,1,0:T(1,128)} %shard_map.20), calls=%async_computation.1 | async-start | bytes 65536 | tf_op jit(solution)/shard_map/all_to_all | solution.py:249
  43.9 6.5 %collective-permute-start = (f32[32,128]{1,0:T(8,128)S(1)}, f32[32,128]{1,0:T(8,128)S(1)}, u32[]{:S(2)}, u32[]{:S(2)}) collective-permute-start(f32[32,128]{1,0:T(8,128)S(1)} %get-tuple-element.15), channel_id=1, source_target_pairs={{0,1},{1,0},{2,3},{3,2},{4,5},{5,4},{6,7},{7,6},{8,9},{9,8},{10,11... | collective-permute-start | bytes 49160 | tf_op jit(solution)/shard_map/ppermute | solution.py:254
  46.3 6.3 %collective-permute-start.1 = (f32[32,128]{1,0:T(8,128)S(1)}, f32[32,128]{1,0:T(8,128)S(1)}, u32[]{:S(2)}, u32[]{:S(2)}) collective-permute-start(f32[32,128]{1,0:T(8,128)S(1)} %get-tuple-element.16), channel_id=1, source_target_pairs={{0,63},{1,2},{2,1},{3,4},{4,3},{5,6},{6,5},{7,8},{8,7},{9,10},{10,... | collective-permute-start | bytes 49160 | tf_op jit(solution)/shard_map/ppermute | solution.py:253

commit v6 on v5

--- a/solution.py
+++ b/solution.py
@@ -9,6 +9,8 @@
 
 ROW = ("row_0", "row_1")
 COL = ("col_0", "col_1", "col_2")
+SIDE = (*ROW, COL[-1])
+REST = COL[:-1]
 
 GAMMA = 1.4
 COURANT = 0.3
@@ -118,7 +120,7 @@
     ends, starts = jnp.concatenate(ends, axis=0), jnp.concatenate(starts, axis=0)
     for j in range(count):
         send_ref[j] = ends
-    send_ref[lax.rem(me_ref[0] // 2 + count - 1, count)] = starts
+    send_ref[lax.rem(me_ref[0] + count - 2, count)] = starts
 
 
 def inner_kernel(cells_ref, change_ref):
@@ -143,8 +145,8 @@
 ):
     count = received_ref.shape[0]
     rows, columns = cells_ref.shape[1:]
-    me, odd = me_ref[0] // 2, lax.rem(me_ref[0], 2) == 1
-    before, after = lax.rem(me + count - 1, count), lax.rem(me + 1, count)
+    me, odd = me_ref[0], lax.rem(me_ref[0], 2) == 1
+    before, after = lax.rem(me + count - 2, count), lax.rem(me + 2, count)
     half = lax.broadcasted_iota(jnp.int32, (1, columns), 1) < rows
     side_ref[0] = received_ref[after]
     side_ref[1] = pltpu.roll(received_ref[after], rows, 1)
@@ -233,20 +235,20 @@
 def local(fields):
     rows, columns = fields.shape[2:]
     fields = fields.reshape(FIELDS, rows, columns)
-    count_row, count_col = lax.axis_size(ROW), lax.axis_size(COL)
-    me = (lax.axis_index(ROW) * 2 + lax.axis_index(COL[-1])).astype(jnp.int32).reshape(1)
+    count_side, count_rest, count_col = lax.axis_size(SIDE), lax.axis_size(REST), lax.axis_size(COL)
+    me = lax.axis_index(SIDE).astype(jnp.int32).reshape(1)
     whole = kept(FIELDS, rows, columns)
     halo = kept(32, columns)
     inside = [(i, i ^ 1) for i in range(count_col)]
     between = [(i, (i + (1 if i % 2 else -1)) % count_col) for i in range(count_col)]
 
-    shapes = (kept(count_row, PACKED, columns), kept(48, columns), whole)
+    shapes = (kept(count_side, PACKED, columns), kept(48, columns), whole)
     scratch = [pltpu.VMEM((48, columns), jnp.float32)]
     send, own, cells = call(start_kernel, shapes, 1, 1, scratch)(me, fields)
-    received = lax.all_to_all(send, ROW, 0, 0, tiled=True)
+    received = lax.all_to_all(send, SIDE, 0, 0, tiled=True)
     inner = call(inner_kernel, whole, 0, 1)(*held(cells))
-    peak = call(peak_kernel, kept(count_col, 1, columns), 0, 1)(*held(received))
-    peaks = lax.all_to_all(peak, COL, 0, 0, tiled=True)
+    peak = call(peak_kernel, kept(count_rest, 1, columns), 0, 1)(*held(received))
+    peaks = lax.all_to_all(peak, REST, 0, 0, tiled=True)
     scratch = [(FIELDS, 16, columns), (4, PACKED, columns), (columns, columns)]
     scratch = [pltpu.VMEM(shape, jnp.float32) for shape in scratch]
     change, near, far = call(edge_kernel, (whole, halo, halo), 1, 4, scratch)(me, *held(cells, inner, own, received))

time: 56.2 us -> 55.9 us (level); the launches traced: 55.9 us -> 54.9 us
  blocking collectives: 18.6 us -> 26.2 us
  starting transfers between devices: 28.9 us -> 21.5 us
  waiting for transfers between devices: 4.34 us -> 3.16 us
    all_to_all x1, starting transfers between devices: 22.4 us -> 14.7 us  [local(): peaks = lax.all_to_all(peak, REST, 0, 0, tiled=True)]
    all_to_all x1, blocking collectives: 18.6 us -> 26.2 us  [local(): received = lax.all_to_all(send, SIDE, 0, 0, tiled=True)]
    all_to_all x1, waiting for transfers between devices: 2.19 us -> 1.13 us  [local(): peaks = lax.all_to_all(peak, REST, 0, 0, tiled=True)]
where the time goes in v6:
time: 55.9 us; the launch traced here: 54.9 us
  blocking collectives  26.2 us (47%)
  starting transfers between devices  21.5 us (38%)
  Pallas kernels  3.96 us (7%)
  waiting for transfers between devices  3.16 us (6%)
    all_to_all x1, blocking collectives, local(): received = lax.all_to_all(send, SIDE, 0, 0, tiled=True)  26.2 us
    all_to_all x1, starting transfers between devices, local(): peaks = lax.all_to_all(peak, REST, 0, 0, tiled=True)  14.7 us
    ppermute x1, starting transfers between devices, local(): far = lax.ppermute(far, COL, between)  4.21 us
    ppermute x1, starting transfers between devices, local(): near = lax.ppermute(near, COL, inside)  2.63 us
    ppermute x1, waiting for transfers between devices, local(): far = lax.ppermute(far, COL, between)  2.02 us
    pallas_call x1, Pallas kernels, local(): send, own, cells = call(start_kernel, shapes, 1, 1, scratch)(me, fields)  1.21 us
    pallas_call x1, Pallas kernels, local(): call(sweep_kernel, f32(FIELDS, rows, columns), 1, 5, scratch)  1.17 us
    all_to_all x1, waiting for transfers between devices, local(): peaks = lax.all_to_all(peak, REST, 0, 0, tiled=True)  1.13 us
  transfers between devices with their start and end apart: 3, of which 2 were waited for; matrix products, arithmetic and copies ran while one was open for 0% of the time, Pallas kernels for 2%

profile of v6, /device:TPU:1, one launch (start us, length us, event | category | flops | bytes accessed | tf_op | source)
XLA Modules:
  0.0 54.9 jit_solution(13776955148863147702)
XLA Ops:
  0.0 1.2 %shard_map.17 = (f32[32,8,128]{2,1,0:T(8,128)S(1)}, f32[48,128]{1,0:T(8,128)S(1)}, f32[5,64,128]{2,1,0:T(8,128)S(1)}) custom-call(s32[1]{0:T(128)} %bitcast.me_ref, f32[5,64,128]{2,1,0:T(8,128)} %bitcast.5), custom_call_target="tpu_custom_call" | custom-call | flops 4000000 | bytes 1000000 | tf_op jit(solution)/shard_map/pallas_call | solution.py:247
  1.2 26.2 %all_to_all.10.received_ref = f32[32,8,128]{2,1,0:T(8,128)S(1)} all-to-all(f32[32,8,128]{2,1,0:T(8,128)S(1)} %get-tuple-element.13), channel_id=1, replica_groups=mesh['row_0'=8,'row_1'=2,'col_0'=8,'col_1'=4,'col_2'=2] {'row_0','row_1'..., dimensions={0} | all-to-all | bytes 262144 | tf_op jit(solution)/shard_map/all_to_all | solution.py:248
  27.4 0.7 %shard_map.20 = f32[32,1,128]{2,1,0:T(1,128)} custom-call(f32[32,8,128]{2,1,0:T(8,128)S(1)} %all_to_all.10.received_ref), custom_call_target="tpu_custom_call" | custom-call | flops 4000000 | bytes 1000000 | tf_op jit(solution)/shard_map/pallas_call | solution.py:250
  28.1 14.7 %all-to-all-start.1 = ((f32[32,1,128]{2,1,0:T(1,128)}), f32[32,1,128]{2,1,0:T(1,128)S(1)}, u32[]{:S(2)}, u32[]{:S(2)}) async-start(f32[32,1,128]{2,1,0:T(1,128)} %shard_map.20), calls=%async_computation.1 | async-start | bytes 32768 | tf_op jit(solution)/shard_map/all_to_all | solution.py:251
  42.8 0.5 shard_map.18.inner_ref
  43.3 0.4 shard_map.19
  43.7 2.6 %collective-permute-start = (f32[32,128]{1,0:T(8,128)S(1)}, f32[32,128]{1,0:T(8,128)S(1)}, u32[]{:S(2)}, u32[]{:S(2)}) collective-permute-start(f32[32,128]{1,0:T(8,128)S(1)} %get-tuple-element.15), channel_id=1, source_target_pairs={{0,1},{1,0},{2,3},{3,2},{4,5},{5,4},{6,7},{7,6},{8,9},{9,8},{10,11... | collective-permute-start | bytes 49160 | tf_op jit(solution)/shard_map/ppermute | solution.py:256
  46.3 4.2 %collective-permute-start.1 = (f32[32,128]{1,0:T(8,128)S(1)}, f32[32,128]{1,0:T(8,128)S(1)}, u32[]{:S(2)}, u32[]{:S(2)}) collective-permute-start(f32[32,128]{1,0:T(8,128)S(1)} %get-tuple-element.16), channel_id=1, source_target_pairs={{0,63},{1,2},{2,1},{3,4},{4,3},{5,6},{6,5},{7,8},{8,7},{9,10},{10,... | collective-permute-start | bytes 49160 | tf_op jit(solution)/shard_map/ppermute | solution.py:255
  50.5 0.0 collective-permute-done.near_ref
  50.5 2.0 %collective-permute-done.1.far_ref = f32[32,128]{1,0:T(8,128)S(1)} collective-permute-done((f32[32,128]{1,0:T(8,128)S(1)}, f32[32,128]{1,0:T(8,128)S(1)}, u32[]{:S(2)}, u32[]{:S(2)}) %collective-permute-start.1) | collective-permute-done | bytes 16416 | tf_op jit(solution)/shard_map/ppermute | solution.py:255
  52.6 1.1 %all-to-all-done.1.peaks_ref = f32[32,1,128]{2,1,0:T(1,128)S(1)} async-done(((f32[32,1,128]{2,1,0:T(1,128)}), f32[32,1,128]{2,1,0:T(1,128)S(1)}, u32[]{:S(2)}, u32[]{:S(2)}) %all-to-all-start.1) | async-done | bytes 16416 | tf_op jit(solution)/shard_map/all_to_all | solution.py:251
  53.7 1.2 %shard_map.21 = f32[5,64,128]{2,1,0:T(8,128)} custom-call(s32[1]{0:T(128)} %bitcast.me_ref, f32[5,64,128]{2,1,0:T(8,128)S(1)} %get-tuple-element.11.cells_ref, f32[5,64,128]{2,1,0:T(8,128)S(1)} %get-tuple-element.14.change_ref, f32[32,1,128]{2,1,0:T(1,128)S(1)} %all-to-all-done.1.peaks_ref, f32[32,128]{1,0:T(8,128)S(1)} %collective-permute-done.near_ref, ...), custom_call_target="tpu_custom_call" | custom-call | flops 4000000 | bytes 1000000 | tf_op jit(solution)/shard_map/pallas_call | solution.py:258
Async XLA Ops:
  28.1 25.6 %all-to-all-start.1 = ((f32[32,1,128]{2,1,0:T(1,128)}), f32[32,1,128]{2,1,0:T(1,128)S(1)}, u32[]{:S(2)}, u32[]{:S(2)}) async-start(f32[32,1,128]{2,1,0:T(1,128)} %shard_map.20), calls=%async_computation.1 | async-start | bytes 32768 | tf_op jit(solution)/shard_map/all_to_all | solution.py:251
  43.7 6.9 %collective-permute-start = (f32[32,128]{1,0:T(8,128)S(1)}, f32[32,128]{1,0:T(8,128)S(1)}, u32[]{:S(2)}, u32[]{:S(2)}) collective-permute-start(f32[32,128]{1,0:T(8,128)S(1)} %get-tuple-element.15), channel_id=1, source_target_pairs={{0,1},{1,0},{2,3},{3,2},{4,5},{5,4},{6,7},{7,6},{8,9},{9,8},{10,11... | collective-permute-start | bytes 49160 | tf_op jit(solution)/shard_map/ppermute | solution.py:256
  46.3 6.3 %collective-permute-start.1 = (f32[32,128]{1,0:T(8,128)S(1)}, f32[32,128]{1,0:T(8,128)S(1)}, u32[]{:S(2)}, u32[]{:S(2)}) collective-permute-start(f32[32,128]{1,0:T(8,128)S(1)} %get-tuple-element.16), channel_id=1, source_target_pairs={{0,63},{1,2},{2,1},{3,4},{4,3},{5,6},{6,5},{7,8},{8,7},{9,10},{10,... | collective-permute-start | bytes 49160 | tf_op jit(solution)/shard_map/ppermute | solution.py:255

commit v7 on v6

--- a/solution.py
+++ b/solution.py
@@ -1,3 +1,5 @@
+import functools
+
 import jax
 import jax.numpy as jnp
 from jax import lax
@@ -9,8 +11,8 @@
 
 ROW = ("row_0", "row_1")
 COL = ("col_0", "col_1", "col_2")
-SIDE = (*ROW, COL[-1])
-REST = COL[:-1]
+SIDE = (COL[-1], *ROW)
+REST = (COL[1], COL[0])
 
 GAMMA = 1.4
 COURANT = 0.3
@@ -80,6 +82,12 @@
     return differences
 
 
+def beside(me, step, count):
+    size = count // 2
+    row = lax.rem(me, size)
+    return me - row + lax.rem(row + size + step, size)
+
+
 def start_kernel(me_ref, fields_ref, send_ref, own_ref, cells_ref, swapped_ref):
     count = send_ref.shape[0]
     rows, columns = fields_ref.shape[1:]
@@ -120,7 +128,7 @@
     ends, starts = jnp.concatenate(ends, axis=0), jnp.concatenate(starts, axis=0)
     for j in range(count):
         send_ref[j] = ends
-    send_ref[lax.rem(me_ref[0] + count - 2, count)] = starts
+    send_ref[beside(me_ref[0], -1, count)] = starts
 
 
 def inner_kernel(cells_ref, change_ref):
@@ -145,8 +153,8 @@
 ):
     count = received_ref.shape[0]
     rows, columns = cells_ref.shape[1:]
-    me, odd = me_ref[0], lax.rem(me_ref[0], 2) == 1
-    before, after = lax.rem(me + count - 2, count), lax.rem(me + 2, count)
+    me, odd = me_ref[0], me_ref[0] >= count // 2
+    before, after = beside(me, -1, count), beside(me, 1, count)
     half = lax.broadcasted_iota(jnp.int32, (1, columns), 1) < rows
     side_ref[0] = received_ref[after]
     side_ref[1] = pltpu.roll(received_ref[after], rows, 1)
@@ -188,12 +196,12 @@
     far_ref[2 * FIELDS * WIDTH :, :] = jnp.zeros((2, columns), jnp.float32)
 
 
-def sweep_kernel(me_ref, cells_ref, change_ref, peaks_ref, near_ref, far_ref, out_ref, half_ref):
+def sweep_kernel(count, me_ref, cells_ref, change_ref, peaks_ref, near_ref, far_ref, out_ref, half_ref):
     rows, _ = out_ref.shape[1:]
     peak = jnp.max(jnp.max(peaks_ref[...], axis=0), axis=1, keepdims=True)
     time_step = COURANT / peak
     size = FIELDS * WIDTH
-    odd = lax.rem(me_ref[0], 2) == 1
+    odd = me_ref[0] >= count // 2
     near = near_ref[:size, :] - time_step * near_ref[size : 2 * size, :]
     far = far_ref[:size, :] - time_step * far_ref[size : 2 * size, :]
     before, after = jnp.where(odd, near, far), jnp.where(odd, far, near)
@@ -255,7 +263,7 @@
     far = lax.ppermute(far, COL, between)
     near = lax.ppermute(near, COL, inside)
     scratch = [pltpu.VMEM((FIELDS, rows + 8, columns), jnp.float32)]
-    out = call(sweep_kernel, f32(FIELDS, rows, columns), 1, 5, scratch)(
+    out = call(functools.partial(sweep_kernel, count_side), f32(FIELDS, rows, columns), 1, 5, scratch)(
         me, *held(cells, change, peaks, near, far)
     )
     return out.reshape(FIELDS, 1, rows, columns)

time: 55.9 us -> 56.1 us (level)
  no operation moved by 1% of the time
where the time goes in v7:
time: 56.1 us; the launch traced here: 55 us
  blocking collectives  26.2 us (47%)
  starting transfers between devices  21.8 us (39%)
  Pallas kernels  3.96 us (7%)
  waiting for transfers between devices  3 us (5%)
    all_to_all x1, blocking collectives, local(): received = lax.all_to_all(send, SIDE, 0, 0, tiled=True)  26.2 us
    all_to_all x1, starting transfers between devices, local(): peaks = lax.all_to_all(peak, REST, 0, 0, tiled=True)  14.8 us
    ppermute x1, starting transfers between devices, local(): far = lax.ppermute(far, COL, between)  4.22 us
    ppermute x1, starting transfers between devices, local(): near = lax.ppermute(near, COL, inside)  2.84 us
    ppermute x1, waiting for transfers between devices, local(): far = lax.ppermute(far, COL, between)  2.02 us
    pallas_call x1, Pallas kernels, local(): send, own, cells = call(start_kernel, shapes, 1, 1, scratch)(me, fields)  1.21 us
    pallas_call x1, Pallas kernels, local(): call(functools.partial(sweep_kernel, count_side), f32(FIELDS, rows, colum...  1.17 us
  transfers between devices with their start and end apart: 3, of which 2 were waited for; matrix products, arithmetic and copies ran while one was open for 0% of the time, Pallas kernels for 2%

profile of v7, /device:TPU:1, one launch (start us, length us, event | category | flops | bytes accessed | tf_op | source)
XLA Modules:
  0.0 55.0 jit_solution(5575349186621162509)
XLA Ops:
  0.0 1.2 %shard_map.17 = (f32[32,8,128]{2,1,0:T(8,128)S(1)}, f32[48,128]{1,0:T(8,128)S(1)}, f32[5,64,128]{2,1,0:T(8,128)S(1)}) custom-call(s32[1]{0:T(128)} %bitcast.me_ref, f32[5,64,128]{2,1,0:T(8,128)} %bitcast.5), custom_call_target="tpu_custom_call" | custom-call | flops 4000000 | bytes 1000000 | tf_op jit(solution)/shard_map/pallas_call | solution.py:255
  1.2 26.2 %all_to_all.10.received_ref = f32[32,8,128]{2,1,0:T(8,128)S(1)} all-to-all(f32[32,8,128]{2,1,0:T(8,128)S(1)} %get-tuple-element.13), channel_id=1, replica_groups=mesh['row_0'=8,'row_1'=2,'col_0'=8,'col_1'=4,'col_2'=2] {'col_2','row_0'..., dimensions={0} | all-to-all | bytes 262144 | tf_op jit(solution)/shard_map/all_to_all | solution.py:256
  27.4 0.7 %shard_map.20 = f32[32,1,128]{2,1,0:T(1,128)} custom-call(f32[32,8,128]{2,1,0:T(8,128)S(1)} %all_to_all.10.received_ref), custom_call_target="tpu_custom_call" | custom-call | flops 4000000 | bytes 1000000 | tf_op jit(solution)/shard_map/pallas_call | solution.py:258
  28.1 14.8 %all-to-all-start.1 = ((f32[32,1,128]{2,1,0:T(1,128)}), f32[32,1,128]{2,1,0:T(1,128)S(1)}, u32[]{:S(2)}, u32[]{:S(2)}) async-start(f32[32,1,128]{2,1,0:T(1,128)} %shard_map.20), calls=%async_computation.1 | async-start | bytes 32768 | tf_op jit(solution)/shard_map/all_to_all | solution.py:259
  42.9 0.5 shard_map.18.inner_ref
  43.4 0.4 shard_map.19
  43.8 2.8 %collective-permute-start = (f32[32,128]{1,0:T(8,128)S(1)}, f32[32,128]{1,0:T(8,128)S(1)}, u32[]{:S(2)}, u32[]{:S(2)}) collective-permute-start(f32[32,128]{1,0:T(8,128)S(1)} %get-tuple-element.15), channel_id=1, source_target_pairs={{0,1},{1,0},{2,3},{3,2},{4,5},{5,4},{6,7},{7,6},{8,9},{9,8},{10,11... | collective-permute-start | bytes 49160 | tf_op jit(solution)/shard_map/ppermute | solution.py:264
  46.6 4.2 %collective-permute-start.1 = (f32[32,128]{1,0:T(8,128)S(1)}, f32[32,128]{1,0:T(8,128)S(1)}, u32[]{:S(2)}, u32[]{:S(2)}) collective-permute-start(f32[32,128]{1,0:T(8,128)S(1)} %get-tuple-element.16), channel_id=1, source_target_pairs={{0,63},{1,2},{2,1},{3,4},{4,3},{5,6},{6,5},{7,8},{8,7},{9,10},{10,... | collective-permute-start | bytes 49160 | tf_op jit(solution)/shard_map/ppermute | solution.py:263
  50.9 0.0 collective-permute-done.near_ref
  50.9 2.0 %collective-permute-done.1.far_ref = f32[32,128]{1,0:T(8,128)S(1)} collective-permute-done((f32[32,128]{1,0:T(8,128)S(1)}, f32[32,128]{1,0:T(8,128)S(1)}, u32[]{:S(2)}, u32[]{:S(2)}) %collective-permute-start.1) | collective-permute-done | bytes 16416 | tf_op jit(solution)/shard_map/ppermute | solution.py:263
  52.9 1.0 %all-to-all-done.1.peaks_ref = f32[32,1,128]{2,1,0:T(1,128)S(1)} async-done(((f32[32,1,128]{2,1,0:T(1,128)}), f32[32,1,128]{2,1,0:T(1,128)S(1)}, u32[]{:S(2)}, u32[]{:S(2)}) %all-to-all-start.1) | async-done | bytes 16416 | tf_op jit(solution)/shard_map/all_to_all | solution.py:259
  53.9 1.2 %shard_map.21 = f32[5,64,128]{2,1,0:T(8,128)} custom-call(s32[1]{0:T(128)} %bitcast.me_ref, f32[5,64,128]{2,1,0:T(8,128)S(1)} %get-tuple-element.11.cells_ref, f32[5,64,128]{2,1,0:T(8,128)S(1)} %get-tuple-element.14.change_ref, f32[32,1,128]{2,1,0:T(1,128)S(1)} %all-to-all-done.1.peaks_ref, f32[32,128]{1,0:T(8,128)S(1)} %collective-permute-done.near_ref, ...), custom_call_target="tpu_custom_call" | custom-call | flops 4000000 | bytes 1000000 | tf_op jit(solution)/shard_map/pallas_call | solution.py:266
Async XLA Ops:
  28.1 25.8 %all-to-all-start.1 = ((f32[32,1,128]{2,1,0:T(1,128)}), f32[32,1,128]{2,1,0:T(1,128)S(1)}, u32[]{:S(2)}, u32[]{:S(2)}) async-start(f32[32,1,128]{2,1,0:T(1,128)} %shard_map.20), calls=%async_computation.1 | async-start | bytes 32768 | tf_op jit(solution)/shard_map/all_to_all | solution.py:259
  43.8 7.1 %collective-permute-start = (f32[32,128]{1,0:T(8,128)S(1)}, f32[32,128]{1,0:T(8,128)S(1)}, u32[]{:S(2)}, u32[]{:S(2)}) collective-permute-start(f32[32,128]{1,0:T(8,128)S(1)} %get-tuple-element.15), channel_id=1, source_target_pairs={{0,1},{1,0},{2,3},{3,2},{4,5},{5,4},{6,7},{7,6},{8,9},{9,8},{10,11... | collective-permute-start | bytes 49160 | tf_op jit(solution)/shard_map/ppermute | solution.py:264
  46.6 6.3 %collective-permute-start.1 = (f32[32,128]{1,0:T(8,128)S(1)}, f32[32,128]{1,0:T(8,128)S(1)}, u32[]{:S(2)}, u32[]{:S(2)}) collective-permute-start(f32[32,128]{1,0:T(8,128)S(1)} %get-tuple-element.16), channel_id=1, source_target_pairs={{0,63},{1,2},{2,1},{3,4},{4,3},{5,6},{6,5},{7,8},{8,7},{9,10},{10,... | collective-permute-start | bytes 49160 | tf_op jit(solution)/shard_map/ppermute | solution.py:263

commit v8 on v5

--- a/solution.py
+++ b/solution.py
@@ -9,6 +9,8 @@
 
 ROW = ("row_0", "row_1")
 COL = ("col_0", "col_1", "col_2")
+FIRST = (ROW[0], COL[0])
+SECOND = (COL[1], ROW[1], COL[2])
 
 GAMMA = 1.4
 COURANT = 0.3
@@ -78,8 +80,7 @@
     return differences
 
 
-def start_kernel(me_ref, fields_ref, send_ref, own_ref, cells_ref, swapped_ref):
-    count = send_ref.shape[0]
+def start_kernel(me_ref, fields_ref, peak_ref, near_ref, far_ref, own_ref, cells_ref, swapped_ref):
     rows, columns = fields_ref.shape[1:]
     cells = [fields_ref[k] for k in range(FIELDS)]
     for k in range(FIELDS):
@@ -88,7 +89,7 @@
     speed = jnp.maximum(jnp.abs(velocity[0]), jnp.abs(velocity[1]))
     speed = speed + jnp.sqrt(GAMMA * pressure / density)
     peak = jnp.max(speed, axis=0, keepdims=True)
-    peak = jnp.maximum(peak, pltpu.roll(peak, rows, 1))
+    peak_ref[...] = jnp.broadcast_to(peak[None], peak_ref.shape)
     lane = lax.broadcasted_iota(jnp.int32, (rows, columns), 1)
     ends = starts = jnp.zeros((rows, columns), jnp.float32)
     for k in range(FIELDS):
@@ -108,17 +109,13 @@
 
     ends, starts = [], []
     for row in range(PACKED):
-        last = row == PACKED - 1
-        ends.append(
-            jnp.where(half, row_of(own_ref, row), peak if last else row_of(swapped_ref, PACKED + row))
-        )
-        starts.append(
-            jnp.where(half, row_of(swapped_ref, row), peak if last else row_of(own_ref, PACKED + row))
-        )
+        high = min(PACKED + row, FIELDS * WIDTH - 1)
+        ends.append(jnp.where(half, row_of(own_ref, row), row_of(swapped_ref, high)))
+        starts.append(jnp.where(half, row_of(swapped_ref, row), row_of(own_ref, high)))
     ends, starts = jnp.concatenate(ends, axis=0), jnp.concatenate(starts, axis=0)
-    for j in range(count):
-        send_ref[j] = ends
-    send_ref[lax.rem(me_ref[0] // 2 + count - 1, count)] = starts
+    odd = me_ref[0] >= 2
+    near_ref[...] = jnp.where(odd, starts, ends)
+    far_ref[...] = jnp.where(odd, ends, starts)
 
 
 def inner_kernel(cells_ref, change_ref):
@@ -129,27 +126,22 @@
 
 
 def peak_kernel(received_ref, peak_ref):
-    columns = received_ref.shape[2]
-    rows = columns // 2
-    half = lax.broadcasted_iota(jnp.int32, (1, columns), 1) < rows
-    peak = jnp.max(received_ref[...], axis=0)[PACKED - 1 :, :]
-    peak = jnp.where(half, pltpu.roll(peak, rows, 1), peak)
-    peak_ref[...] = jnp.broadcast_to(peak[None], peak_ref.shape)
+    peak_ref[...] = jnp.broadcast_to(jnp.max(received_ref[...], axis=0)[None], peak_ref.shape)
 
 
 def edge_kernel(
-    me_ref, cells_ref, inner_ref, own_ref, received_ref,
+    me_ref, cells_ref, inner_ref, own_ref, near_side_ref, far_side_ref,
     change_ref, near_ref, far_ref, strip_ref, side_ref, turned_ref,
 ):
-    count = received_ref.shape[0]
     rows, columns = cells_ref.shape[1:]
-    me, odd = me_ref[0] // 2, lax.rem(me_ref[0], 2) == 1
-    before, after = lax.rem(me + count - 1, count), lax.rem(me + 1, count)
+    odd_row, odd = me_ref[0] >= 2, lax.rem(me_ref[0], 2) == 1
     half = lax.broadcasted_iota(jnp.int32, (1, columns), 1) < rows
-    side_ref[0] = received_ref[after]
-    side_ref[1] = pltpu.roll(received_ref[after], rows, 1)
-    side_ref[2] = received_ref[before]
-    side_ref[3] = pltpu.roll(received_ref[before], rows, 1)
+    after = jnp.where(odd_row, far_side_ref[...], near_side_ref[...])
+    before = jnp.where(odd_row, near_side_ref[...], far_side_ref[...])
+    side_ref[0] = after
+    side_ref[1] = pltpu.roll(after, rows, 1)
+    side_ref[2] = before
+    side_ref[3] = pltpu.roll(before, rows, 1)
     for k in range(FIELDS):
         at = k * STRIP
         strip_ref[k, :STRIP, :] = own_ref[at : at + STRIP, :]
@@ -233,23 +225,32 @@
 def local(fields):
     rows, columns = fields.shape[2:]
     fields = fields.reshape(FIELDS, rows, columns)
-    count_row, count_col = lax.axis_size(ROW), lax.axis_size(COL)
-    me = (lax.axis_index(ROW) * 2 + lax.axis_index(COL[-1])).astype(jnp.int32).reshape(1)
+    count_first, count_second = lax.axis_size(FIRST), lax.axis_size(SECOND)
+    me = (lax.axis_index(ROW[1]) * 2 + lax.axis_index(COL[2])).astype(jnp.int32).reshape(1)
     whole = kept(FIELDS, rows, columns)
-    halo = kept(32, columns)
-    inside = [(i, i ^ 1) for i in range(count_col)]
-    between = [(i, (i + (1 if i % 2 else -1)) % count_col) for i in range(count_col)]
-
-    shapes = (kept(count_row, PACKED, columns), kept(48, columns), whole)
+    halo, side = kept(32, columns), kept(PACKED, columns)
+
+    def pairings(axes):
+        count = lax.axis_size(axes)
+        near = [(i, i ^ 1) for i in range(count)]
+        return near, [(i, (i + (1 if i % 2 else -1)) % count) for i in range(count)]
+
+    inside_row, between_row = pairings(ROW)
+    inside, between = pairings(COL)
+    shapes = (kept(count_first, 1, columns), side, side, kept(48, columns), whole)
     scratch = [pltpu.VMEM((48, columns), jnp.float32)]
-    send, own, cells = call(start_kernel, shapes, 1, 1, scratch)(me, fields)
-    received = lax.all_to_all(send, ROW, 0, 0, tiled=True)
+    peak, near_side, far_side, own, cells = call(start_kernel, shapes, 1, 1, scratch)(me, fields)
+    received = lax.all_to_all(peak, FIRST, 0, 0, tiled=True)
+    far_side = lax.ppermute(far_side, ROW, between_row)
+    near_side = lax.ppermute(near_side, ROW, inside_row)
     inner = call(inner_kernel, whole, 0, 1)(*held(cells))
-    peak = call(peak_kernel, kept(count_col, 1, columns), 0, 1)(*held(received))
-    peaks = lax.all_to_all(peak, COL, 0, 0, tiled=True)
+    peak = call(peak_kernel, kept(count_second, 1, columns), 0, 1)(*held(received))
+    peaks = lax.all_to_all(peak, SECOND, 0, 0, tiled=True)
     scratch = [(FIELDS, 16, columns), (4, PACKED, columns), (columns, columns)]
     scratch = [pltpu.VMEM(shape, jnp.float32) for shape in scratch]
-    change, near, far = call(edge_kernel, (whole, halo, halo), 1, 4, scratch)(me, *held(cells, inner, own, received))
+    change, near, far = call(edge_kernel, (whole, halo, halo), 1, 5, scratch)(
+        me, *held(cells, inner, own, near_side, far_side)
+    )
     far = lax.ppermute(far, COL, between)
     near = lax.ppermute(near, COL, inside)
     scratch = [pltpu.VMEM((FIELDS, rows + 8, columns), jnp.float32)]

time: 56.2 us -> 62.1 us (1.10)
  starting transfers between devices: 28.9 us -> 48.1 us
  blocking collectives: 18.6 us -> 0 us
  waiting for transfers between devices: 4.34 us -> 9.13 us
    all_to_all x1 -> x0, blocking collectives: 18.6 us -> none  [local(): received = lax.all_to_all(send, ROW, 0, 0, tiled=True)]
    ppermute x0 -> x2, starting transfers between devices: none -> 9.03 us  [the longest x1 4.91 us: local(): near_side = lax.ppermute(near_side, ROW, inside_row)]
    all_to_all x1 -> x2, starting transfers between devices: 22.4 us -> 27.6 us  [the longest x1 14 us: local(): received = lax.all_to_all(peak, FIRST, 0, 0, tiled=True)]
    all_to_all x1 -> x2, waiting for transfers between devices: 2.19 us -> 7 us  [the longest x1 6.99 us: local(): peaks = lax.all_to_all(peak, SECOND, 0, 0, tiled=True)]
    ppermute x1, starting transfers between devices: 4.1 us -> 6.69 us  [local(): far = lax.ppermute(far, COL, between)]
    ppermute x1, starting transfers between devices: 2.36 us -> 4.83 us  [local(): near = lax.ppermute(near, COL, inside)]
    ppermute x1, waiting for transfers between devices: 2.14 us -> 0.01 us  [local(): far = lax.ppermute(far, COL, between)]
    ppermute x0 -> x2, waiting for transfers between devices: none -> 2.12 us  [the longest x1 2.12 us: local(): far_side = lax.ppermute(far_side, ROW, between_row)]
  transfers between devices with their start and end apart: 3 -> 6, of which waited for: 2 -> 2; matrix products, arithmetic and copies ran while one was open for 0% -> 0% of each run, Pallas kernels for 2% -> 2%
where the time goes in v8:
time: 62.1 us; the launch traced here: 61.8 us
  starting transfers between devices  48.1 us (77%)
  waiting for transfers between devices  9.13 us (15%)
  Pallas kernels  4.43 us (7%)
    all_to_all x1, starting transfers between devices, local(): received = lax.all_to_all(peak, FIRST, 0, 0, tiled=True)  14 us
    all_to_all x1, starting transfers between devices, local(): peaks = lax.all_to_all(peak, SECOND, 0, 0, tiled=True)  13.6 us
    all_to_all x1, waiting for transfers between devices, local(): peaks = lax.all_to_all(peak, SECOND, 0, 0, tiled=True)  6.99 us
    ppermute x1, starting transfers between devices, local(): far = lax.ppermute(far, COL, between)  6.69 us
    ppermute x1, starting transfers between devices, local(): near_side = lax.ppermute(near_side, ROW, inside_row)  4.91 us
    ppermute x1, starting transfers between devices, local(): near = lax.ppermute(near, COL, inside)  4.83 us
    ppermute x1, starting transfers between devices, local(): far_side = lax.ppermute(far_side, ROW, between_row)  4.12 us
    ppermute x1, waiting for transfers between devices, local(): far_side = lax.ppermute(far_side, ROW, between_row)  2.12 us
  transfers between devices with their start and end apart: 6, of which 2 were waited for; matrix products, arithmetic and copies ran while one was open for 0% of the time, Pallas kernels for 2%

profile of v8, /device:TPU:1, one launch (start us, length us, event | category | flops | bytes accessed | tf_op | source)
XLA Modules:
  0.0 61.8 jit_solution(7510377928351368582)
XLA Ops:
  0.0 1.8 %shard_map.17 = (f32[64,1,128]{2,1,0:T(1,128)}, f32[8,128]{1,0:T(8,128)S(1)}, f32[8,128]{1,0:T(8,128)S(1)}, f32[48,128]{1,0:T(8,128)S(1)}, f32[5,64,128]{2,1,0:T(8,128)S(1)}) custom-call(s32[1]{0:T(128)} %bitcast.me_ref, f32[5,64,128]{2,1,0:T(8,128)} %bitcast.5), custom_call_target="tpu_custom_call" | custom-call | flops 4000000 | bytes 1000000 | tf_op jit(solution)/shard_map/pallas_call | solution.py:242
  1.8 14.0 %all-to-all-start = ((f32[64,1,128]{2,1,0:T(1,128)}), f32[64,1,128]{2,1,0:T(1,128)S(1)}, u32[]{:S(2)}, u32[]{:S(2)}) async-start(f32[64,1,128]{2,1,0:T(1,128)} %get-tuple-element.18), calls=%async_computation | async-start | bytes 65536 | tf_op jit(solution)/shard_map/all_to_all | solution.py:243
  15.8 4.9 %collective-permute-start = (f32[8,128]{1,0:T(8,128)S(1)}, f32[8,128]{1,0:T(8,128)S(1)}, u32[]{:S(2)}, u32[]{:S(2)}) collective-permute-start(f32[8,128]{1,0:T(8,128)S(1)} %get-tuple-element.15), channel_id=1, source_target_pairs={{0,64},{64,0},{128,192},{192,128},{256,320},{320,256},{384,448},{4... | collective-permute-start | bytes 12296 | tf_op jit(solution)/shard_map/ppermute | solution.py:245
  20.7 4.1 %collective-permute-start.1 = (f32[8,128]{1,0:T(8,128)S(1)}, f32[8,128]{1,0:T(8,128)S(1)}, u32[]{:S(2)}, u32[]{:S(2)}) collective-permute-start(f32[8,128]{1,0:T(8,128)S(1)} %get-tuple-element.16), channel_id=1, source_target_pairs={{0,960},{64,128},{128,64},{192,256},{256,192},{320,384},{384,320},... | collective-permute-start | bytes 12296 | tf_op jit(solution)/shard_map/ppermute | solution.py:244
  24.8 0.5 shard_map.18.inner_ref
  25.3 0.0 collective-permute-done.near_side_ref
  25.3 2.1 %collective-permute-done.1.far_side_ref = f32[8,128]{1,0:T(8,128)S(1)} collective-permute-done((f32[8,128]{1,0:T(8,128)S(1)}, f32[8,128]{1,0:T(8,128)S(1)}, u32[]{:S(2)}, u32[]{:S(2)}) %collective-permute-start.1) | collective-permute-done | bytes 4128 | tf_op jit(solution)/shard_map/ppermute | solution.py:244
  27.5 0.4 shard_map.19
  27.9 4.8 %collective-permute-start.2 = (f32[32,128]{1,0:T(8,128)S(1)}, f32[32,128]{1,0:T(8,128)S(1)}, u32[]{:S(2)}, u32[]{:S(2)}) collective-permute-start(f32[32,128]{1,0:T(8,128)S(1)} %get-tuple-element.19), channel_id=1, source_target_pairs={{0,1},{1,0},{2,3},{3,2},{4,5},{5,4},{6,7},{7,6},{8,9},{9,8},{10,11... | collective-permute-start | bytes 49160 | tf_op jit(solution)/shard_map/ppermute | solution.py:255
  32.7 6.7 %collective-permute-start.3 = (f32[32,128]{1,0:T(8,128)S(1)}, f32[32,128]{1,0:T(8,128)S(1)}, u32[]{:S(2)}, u32[]{:S(2)}) collective-permute-start(f32[32,128]{1,0:T(8,128)S(1)} %get-tuple-element.20), channel_id=1, source_target_pairs={{0,63},{1,2},{2,1},{3,4},{4,3},{5,6},{6,5},{7,8},{8,7},{9,10},{10,... | collective-permute-start | bytes 49160 | tf_op jit(solution)/shard_map/ppermute | solution.py:254
  39.4 0.0 all-to-all-done.received_ref
  39.4 0.6 %shard_map.20 = f32[16,1,128]{2,1,0:T(1,128)} custom-call(f32[64,1,128]{2,1,0:T(1,128)S(1)} %all-to-all-done.received_ref), custom_call_target="tpu_custom_call" | custom-call | flops 4000000 | bytes 1000000 | tf_op jit(solution)/shard_map/pallas_call | solution.py:247
  40.0 13.6 %all-to-all-start.1 = ((f32[16,1,128]{2,1,0:T(1,128)}), f32[16,1,128]{2,1,0:T(1,128)S(1)}, u32[]{:S(2)}, u32[]{:S(2)}) async-start(f32[16,1,128]{2,1,0:T(1,128)} %shard_map.20), calls=%async_computation.1 | async-start | bytes 16384 | tf_op jit(solution)/shard_map/all_to_all | solution.py:248
  53.6 0.0 collective-permute-done.2.near_ref
  53.6 0.0 collective-permute-done.3.far_ref
  53.6 7.0 %all-to-all-done.1.peaks_ref = f32[16,1,128]{2,1,0:T(1,128)S(1)} async-done(((f32[16,1,128]{2,1,0:T(1,128)}), f32[16,1,128]{2,1,0:T(1,128)S(1)}, u32[]{:S(2)}, u32[]{:S(2)}) %all-to-all-start.1) | async-done | bytes 8224 | tf_op jit(solution)/shard_map/all_to_all | solution.py:248
  60.6 1.2 %shard_map.21 = f32[5,64,128]{2,1,0:T(8,128)} custom-call(s32[1]{0:T(128)} %bitcast.me_ref, f32[5,64,128]{2,1,0:T(8,128)S(1)} %get-tuple-element.13.cells_ref, f32[5,64,128]{2,1,0:T(8,128)S(1)} %get-tuple-element.17.change_ref, f32[16,1,128]{2,1,0:T(1,128)S(1)} %all-to-all-done.1.peaks_ref, f32[32,128]{1,0:T(8,128)S(1)} %collective-permute-done.2.near_ref, ...), custom_call_target="tpu_custom_call" | custom-call | flops 4000000 | bytes 1000000 | tf_op jit(solution)/shard_map/pallas_call | solution.py:257
Async XLA Ops:
  1.8 37.7 %all-to-all-start = ((f32[64,1,128]{2,1,0:T(1,128)}), f32[64,1,128]{2,1,0:T(1,128)S(1)}, u32[]{:S(2)}, u32[]{:S(2)}) async-start(f32[64,1,128]{2,1,0:T(1,128)} %get-tuple-element.18), calls=%async_computation | async-start | bytes 65536 | tf_op jit(solution)/shard_map/all_to_all | solution.py:243
  15.8 9.5 %collective-permute-start = (f32[8,128]{1,0:T(8,128)S(1)}, f32[8,128]{1,0:T(8,128)S(1)}, u32[]{:S(2)}, u32[]{:S(2)}) collective-permute-start(f32[8,128]{1,0:T(8,128)S(1)} %get-tuple-element.15), channel_id=1, source_target_pairs={{0,64},{64,0},{128,192},{192,128},{256,320},{320,256},{384,448},{4... | collective-permute-start | bytes 12296 | tf_op jit(solution)/shard_map/ppermute | solution.py:245
  20.7 6.8 %collective-permute-start.1 = (f32[8,128]{1,0:T(8,128)S(1)}, f32[8,128]{1,0:T(8,128)S(1)}, u32[]{:S(2)}, u32[]{:S(2)}) collective-permute-start(f32[8,128]{1,0:T(8,128)S(1)} %get-tuple-element.16), channel_id=1, source_target_pairs={{0,960},{64,128},{128,64},{192,256},{256,192},{320,384},{384,320},... | collective-permute-start | bytes 12296 | tf_op jit(solution)/shard_map/ppermute | solution.py:244
  27.9 25.7 %collective-permute-start.2 = (f32[32,128]{1,0:T(8,128)S(1)}, f32[32,128]{1,0:T(8,128)S(1)}, u32[]{:S(2)}, u32[]{:S(2)}) collective-permute-start(f32[32,128]{1,0:T(8,128)S(1)} %get-tuple-element.19), channel_id=1, source_target_pairs={{0,1},{1,0},{2,3},{3,2},{4,5},{5,4},{6,7},{7,6},{8,9},{9,8},{10,11... | collective-permute-start | bytes 49160 | tf_op jit(solution)/shard_map/ppermute | solution.py:255
  32.7 20.9 %collective-permute-start.3 = (f32[32,128]{1,0:T(8,128)S(1)}, f32[32,128]{1,0:T(8,128)S(1)}, u32[]{:S(2)}, u32[]{:S(2)}) collective-permute-start(f32[32,128]{1,0:T(8,128)S(1)} %get-tuple-element.20), channel_id=1, source_target_pairs={{0,63},{1,2},{2,1},{3,4},{4,3},{5,6},{6,5},{7,8},{8,7},{9,10},{10,... | collective-permute-start | bytes 49160 | tf_op jit(solution)/shard_map/ppermute | solution.py:254
  40.0 20.6 %all-to-all-start.1 = ((f32[16,1,128]{2,1,0:T(1,128)}), f32[16,1,128]{2,1,0:T(1,128)S(1)}, u32[]{:S(2)}, u32[]{:S(2)}) async-start(f32[16,1,128]{2,1,0:T(1,128)} %shard_map.20), calls=%async_computation.1 | async-start | bytes 16384 | tf_op jit(solution)/shard_map/all_to_all | solution.py:248
